TPU v7x, 128 devices: a whole 4x4x4 slice. The times are simulated.
128 devices in a mesh: sec: 8 (over z_hi, y), tile: 16 (over x, z_lo, core).
Axes of the slice: x: 4, y: 4, z: 4 (z_hi: 2, z_lo: 2; z = z_hi * 2 + z_lo), core: 2. Of those that a mesh axis runs over, the one named last changes fastest.
Arguments:
- patches: bfloat16 [8, 2048, 160, 160], P('sec', 'tile'), may hold values from -6 to 6
- counts: int32 [8, 16], P('sec', 'tile'), may hold values from 16 to 128, as said below
- peak_shifts: int32 [8, 2, 2048], P('sec', None, 'tile'), may hold values from -3 to 3
- mesh_prior: float32 [8, 16, 2, 128, 128], P('sec', 'tile'), may hold values from -6 to 6
Outputs:
- pair_flows: float32 [8, 2, 2048], P('sec', None, 'tile')
- displacement: float32 [8, 16, 2, 128, 128], P('sec', 'tile')
Inputs may be any that keep to these rules, and one draw needn't show every extreme that they name: Slots 0 to counts - 1 of a tile are live. Some tile of every draw has all 128 slots live.
All inputs are finite; a program needn't handle non-finite values.
Results may differ from a plain program's by a relative error of at most 0.0014.
Values may be sent and summed in bfloat16 or wider, within the bound.
A program may use at most 192 MiB of HBM per device.

v0:
```python
import jax
import jax.numpy as jnp
from jax import lax
from jax.sharding import PartitionSpec as P

PCOLS = 16
ITERS = 8


stiffness = 1.0
pull_weight = 4.0
relaxation = 0.8
highest = lax.Precision.HIGHEST


def passed_along(block, axis, distance):
    devices = range(lax.axis_size(axis))
    route = [(i - distance, i) for i in devices if i - distance in devices]
    return lax.ppermute(block, axis, route)


def dft_tables(extent):
    freq_index = jnp.arange(extent, dtype=jnp.int32)
    phases = (
        2.0
        * jnp.pi
        / extent
        * jnp.mod(freq_index[:, None] * freq_index[None, :], extent).astype(jnp.float32)
    )
    cosine_part = jnp.cos(phases)
    sine_part = jnp.sin(phases)
    left_table = jnp.concatenate([cosine_part, sine_part], 0).astype(jnp.bfloat16)
    right_table = jnp.concatenate([cosine_part, -sine_part], 1).astype(jnp.bfloat16)
    return (left_table, right_table)


def row_transform(images, right_table):
    return jnp.einsum(
        "bmn,nk->bmk", images, right_table, preferred_element_type=jnp.float32
    ).astype(jnp.bfloat16)


def column_transform(halfway, left_table):
    extent = halfway.shape[1]
    spectra_all = jnp.einsum("jm,bmk->bjk", left_table, halfway, preferred_element_type=jnp.float32)
    real_part = spectra_all[:, :extent, :extent] + spectra_all[:, extent:, extent:]
    imag_part = spectra_all[:, :extent, extent:] - spectra_all[:, extent:, :extent]
    return (real_part, imag_part)


def window_flows(real_a, imag_a, real_b, imag_b, offsets):
    extent = real_a.shape[-1]
    cross_real = real_a * real_b + imag_a * imag_b
    cross_imag = real_a * imag_b - imag_a * real_b
    freq_index = jnp.arange(extent, dtype=jnp.int32)
    offsets_near = jnp.arange(3, dtype=jnp.int32) - 1

    def waves(shifts):
        lag_values = shifts[:, None] + offsets_near[None, :]
        phases = (
            2.0
            * jnp.pi
            / extent
            * jnp.mod(lag_values[:, :, None] * freq_index[None, None, :], extent).astype(
                jnp.float32
            )
        )
        return (jnp.cos(phases), jnp.sin(phases))

    row_cosine, row_sine = waves(offsets[0])
    col_cosine, col_sine = waves(offsets[1])
    inner_real = jnp.einsum("bkl,bcl->bkc", cross_real, col_cosine, precision=highest) - jnp.einsum(
        "bkl,bcl->bkc", cross_imag, col_sine, precision=highest
    )
    inner_imag = jnp.einsum("bkl,bcl->bkc", cross_real, col_sine, precision=highest) + jnp.einsum(
        "bkl,bcl->bkc", cross_imag, col_cosine, precision=highest
    )
    scores = (
        jnp.einsum("bak,bkc->bac", row_cosine, inner_real, precision=highest)
        - jnp.einsum("bak,bkc->bac", row_sine, inner_imag, precision=highest)
    ) / float(extent) ** 3
    weights = scores * scores
    totals = 1.0 + jnp.sum(weights, axis=(1, 2))
    lag_float = offsets_near.astype(jnp.float32)
    shift_rows = jnp.sum(weights * lag_float[None, :, None], axis=(1, 2)) / totals
    shift_cols = jnp.sum(weights * lag_float[None, None, :], axis=(1, 2)) / totals
    return jnp.stack(
        [offsets[0].astype(jnp.float32) + shift_rows, offsets[1].astype(jnp.float32) + shift_cols],
        0,
    )


def tile_flows(pair_spectra, offsets, live_count, slots, block_size):

    def step(block_index, totals):
        start = (block_index * block_size).astype(jnp.int32)
        real_a, imag_a, real_b, imag_b = pair_spectra(start)
        picked = lax.dynamic_slice_in_dim(offsets, start, block_size, 1)
        return lax.dynamic_update_slice_in_dim(
            totals, window_flows(real_a, imag_a, real_b, imag_b, picked), start, 1
        )

    count_blocks = (live_count + block_size - 1) // block_size
    return lax.fori_loop(0, count_blocks, step, jnp.zeros((2, slots), jnp.float32))


def spread_nodes(values, node_rows, node_cols):
    slots = values.shape[-1]
    patch_rows = slots // PCOLS
    leading = values.shape[:-1]
    shaped = values.reshape(leading + (patch_rows, 1, PCOLS, 1))
    widths = [(0, 0)] * len(leading) + [
        (0, 0),
        (0, node_rows // patch_rows - 1),
        (0, 0),
        (0, node_cols // PCOLS - 1),
    ]
    return jnp.pad(shaped, widths).reshape(leading + (node_rows, node_cols))


def relax_update(moving, padded, target, weight):
    beside = (
        padded[..., :-2, 1:-1]
        + padded[..., 2:, 1:-1]
        + padded[..., 1:-1, :-2]
        + padded[..., 1:-1, 2:]
    )
    pulling = pull_weight * weight[..., None, :, :]
    return moving + relaxation * (
        stiffness * (beside - 4.0 * moving) + pulling * (target - moving)
    ) / (4.0 * stiffness + pulling)


def extend(values, rim_width):
    west_part = passed_along(values[..., -rim_width:], "tile", 1)
    east_part = passed_along(values[..., :rim_width], "tile", -1)
    widened = jnp.concatenate([west_part, values, east_part], -1)
    widths = [(0, 0)] * (widened.ndim - 2) + [(rim_width, rim_width), (0, 0)]
    return jnp.pad(widened, widths)


def body(patches, counts, peak_shifts, mesh_prior):
    extent = patches.shape[-1]
    left_table, right_table = dft_tables(extent)
    current = patches[0]
    slots = current.shape[0]
    block_size = min(32, slots)
    live_count = counts[0, 0]
    positions = jnp.arange(slots, dtype=jnp.int32)

    def take(values, start):
        return lax.dynamic_slice_in_dim(values, start, block_size, 0)

    following = passed_along(current, "sec", -1)

    def pair_spectra(start):
        images = jnp.concatenate([take(current, start), take(following, start)], 0)
        real_part, imag_part = column_transform(row_transform(images, right_table), left_table)
        return (
            real_part[:block_size],
            imag_part[:block_size],
            real_part[block_size:],
            imag_part[block_size:],
        )

    raw_flows = tile_flows(pair_spectra, peak_shifts[0], live_count, slots, block_size)
    live_mask = positions < live_count
    flows_out = jnp.where(live_mask[None, :], raw_flows, 0.0)
    node_rows = mesh_prior.shape[-2]
    node_cols = mesh_prior.shape[-1]
    target = spread_nodes(flows_out, node_rows, node_cols)
    weight = spread_nodes(live_mask.astype(jnp.float32)[None, :], node_rows, node_cols)[0]
    moving = mesh_prior[0, 0]
    halo_depth = ITERS
    tile_count = lax.axis_size("tile")
    column = lax.axis_index("tile")
    stacked = jnp.concatenate([moving, target, weight[None]], 0)
    widened = extend(stacked, halo_depth)
    local_rows = jnp.arange(node_rows + 2 * halo_depth, dtype=jnp.int32) - halo_depth
    global_cols = (
        column * node_cols - halo_depth + jnp.arange(node_cols + 2 * halo_depth, dtype=jnp.int32)
    )
    inside_rows = (local_rows >= 0) & (local_rows < node_rows)
    inside_cols = (global_cols >= 0) & (global_cols < tile_count * node_cols)
    inside = (inside_rows[:, None] & inside_cols[None, :]).astype(jnp.float32)
    widened_moving = widened[:2]
    goal_field = widened[2:4]
    pull_field = widened[4]
    for sweep in range(ITERS):
        padded = jnp.pad(widened_moving, ((0, 0), (1, 1), (1, 1)))
        widened_moving = relax_update(widened_moving, padded, goal_field, pull_field) * inside
    moving = widened_moving[
        :, halo_depth : halo_depth + node_rows, halo_depth : halo_depth + node_cols
    ]
    return (flows_out[None], moving[None, None])


def solution(mesh):
    placed = (
        P("sec", "tile", None, None),
        P("sec", "tile"),
        P("sec", None, "tile"),
        P("sec", "tile", None, None, None),
    )
    return jax.shard_map(
        body,
        mesh=mesh,
        in_specs=placed,
        out_specs=(P("sec", None, "tile"), P("sec", "tile", None, None, None)),
        check_vma=False,
    )
```

profile of v0, /device:TPU:1, one launch (start us, length us, event | category | flops | bytes accessed | tf_op | source)
XLA Modules:
  0.0 427.9 jit_solution(8135149540538141658)
XLA Ops:
  0.6 1.3 collective-permute-start
  2.6 15.0 %copy.18 = bf16[128,160,160]{2,1,0:T(8,128)(2,1)} copy(bf16[128,160,160]{0,2,1:T(8,128)(2,1)} %bitcast.69) | data formatting | bytes 13107200 | tf_op jit(solution)/shard_map/while | solution.py:104
  17.6 0.6 negate_convert_fusion
  18.2 0.7 cosine_convert_fusion
  19.2 0.8 reshape.202
  20.0 0.8 copy.21
  20.9 0.6 copy-done
  21.5 0.7 slice.231
  22.2 0.6 iota_compare_fusion.2
  22.9 122.5 %collective-permute-done = bf16[128,160,160]{0,2,1:T(8,128)(2,1)} collective-permute-done((bf16[128,160,160]{0,2,1:T(8,128)(2,1)}, bf16[128,160,160]{0,2,1:T(8,128)(2,1)}, u32[]{:S(2)}, u32[]{:S(2)}) %collective-permute-start) | collective-permute-done | bytes 6553632 | tf_op jit(solution)/shard_map/ppermute | solution.py:19
  145.5 15.0 %copy.19 = bf16[128,160,160]{2,1,0:T(8,128)(2,1)} copy(bf16[128,160,160]{0,2,1:T(8,128)(2,1)} %collective-permute-done) | data formatting | bytes 13107200 | tf_op jit(solution)/shard_map/while | solution.py:104
  160.5 128.8 %while.12 = (s32[]{:T(128)}, f32[2,128]{1,0:T(2,128)S(1)}, s32[]{:T(128)}, s32[2,128]{1,0:T(2,128)S(1)}, bf16[128,160,160]{2,1,0:T(8,128)(2,1)}, /*index=5*/bf16...) while((s32[]{:T(128)}, f32[2,128]{1,0:T(2,128)S(1)}, ...), condition=%wide.region_4.5_spmd, body=%wide.region_0.4_spmd.sunk | while | flops 3278768896 | bytes 108839896 | solution.py:104
  160.7 4.4 %constant_dynamic-slice_fusion.5 = (bf16[32,160,160]{2,1,0:T(8,128)(2,1)S(1)}, bf16[32,160,160]{2,1,0:T(8,128)(2,1)}) fusion(bf16[128,160,160]{2,1,0:T(8,128)(2,1)} %get-tuple-element.289, s32[]{:T(128)S(6)} %select_n.107, bf16[128,160,160]{2,1,0:T(8,128)(2,1)} %get-tuple-element.288), kind=kLoop, calls=%fused_computation.48.clone.1 | loop fusion | bytes 6553604 | tf_op jit(solution)/shard_map/while/body/dynamic_slice | solution.py:152
  165.1 16.3 %convolution_bitcast_fusion.2 = f32[64,320,320]{1,2,0:T(8,128)} fusion(bf16[32,160,160]{2,1,0:T(8,128)(2,1)S(1)} %get-tuple-element.245, bf16[32,160,160]{2,1,0:T(8,128)(2,1)} %get-tuple-element.246, bf16[320,160]{0,1:T(8,128)(2,1)S(1)} %get-tuple-element.291, bf16[160,320]{1,0:T(8,128)(2,1)S(1)} %get-tuple-element.290), kind=kOutput, calls=%fused_computation.clone.1 | convolution fusion | flops 3150643200 | bytes 29696000 | tf_op jit(solution)/shard_map/while/body/jm,bmk->bjk/dot_general | solution.py:45
  181.5 19.6 %slice_add_fusion.4 = (f32[64,160,160]{1,2,0:T(8,128)S(1)}, f32[64,160,160]{1,2,0:T(8,128)}) fusion(f32[64,320,320]{1,2,0:T(8,128)} %convolution_bitcast_fusion.2), kind=kLoop, calls=%fused_computation.2.clone.1 | loop fusion | flops 3276800 | bytes 39321600 | tf_op jit(solution)/shard_map/while/body/add | solution.py:46
  201.1 4.9 %multiply_subtract_fusion.2 = (f32[32,160,160]{1,2,0:T(8,128)S(1)}, f32[32,160,160]{1,2,0:T(8,128)S(1)}) fusion(f32[64,160,160]{1,2,0:T(8,128)} %get-tuple-element.247, f32[64,160,160]{1,2,0:T(8,128)S(1)} %get-tuple-element.248), kind=kLoop, calls=%fused_computation.8.clone.1 | loop fusion | flops 4915200 | bytes 19660800 | tf_op jit(solution)/shard_map/while/body/sub | solution.py:54
  206.2 3.8 fusion.123
  210.0 3.8 convolution_add_fusion.2
  213.9 3.8 fusion.121
  217.7 3.8 convolution_subtract_fusion.3
  221.5 1.4 fusion.122
  223.0 1.7 multiply_reduce_fusion.3
  224.9 4.4 %constant_dynamic-slice_fusion.5 = (bf16[32,160,160]{2,1,0:T(8,128)(2,1)S(1)}, bf16[32,160,160]{2,1,0:T(8,128)(2,1)}) fusion(bf16[128,160,160]{2,1,0:T(8,128)(2,1)} %get-tuple-element.289, s32[]{:T(128)S(6)} %select_n.107, bf16[128,160,160]{2,1,0:T(8,128)(2,1)} %get-tuple-element.288), kind=kLoop, calls=%fused_computation.48.clone.1 | loop fusion | bytes 6553604 | tf_op jit(solution)/shard_map/while/body/dynamic_slice | solution.py:152
  229.3 16.3 %convolution_bitcast_fusion.2 = f32[64,320,320]{1,2,0:T(8,128)} fusion(bf16[32,160,160]{2,1,0:T(8,128)(2,1)S(1)} %get-tuple-element.245, bf16[32,160,160]{2,1,0:T(8,128)(2,1)} %get-tuple-element.246, bf16[320,160]{0,1:T(8,128)(2,1)S(1)} %get-tuple-element.291, bf16[160,320]{1,0:T(8,128)(2,1)S(1)} %get-tuple-element.290), kind=kOutput, calls=%fused_computation.clone.1 | convolution fusion | flops 3150643200 | bytes 29696000 | tf_op jit(solution)/shard_map/while/body/jm,bmk->bjk/dot_general | solution.py:45
  245.6 19.6 %slice_add_fusion.4 = (f32[64,160,160]{1,2,0:T(8,128)S(1)}, f32[64,160,160]{1,2,0:T(8,128)}) fusion(f32[64,320,320]{1,2,0:T(8,128)} %convolution_bitcast_fusion.2), kind=kLoop, calls=%fused_computation.2.clone.1 | loop fusion | flops 3276800 | bytes 39321600 | tf_op jit(solution)/shard_map/while/body/add | solution.py:46
  265.2 4.9 %multiply_subtract_fusion.2 = (f32[32,160,160]{1,2,0:T(8,128)S(1)}, f32[32,160,160]{1,2,0:T(8,128)S(1)}) fusion(f32[64,160,160]{1,2,0:T(8,128)} %get-tuple-element.247, f32[64,160,160]{1,2,0:T(8,128)S(1)} %get-tuple-element.248), kind=kLoop, calls=%fused_computation.8.clone.1 | loop fusion | flops 4915200 | bytes 19660800 | tf_op jit(solution)/shard_map/while/body/sub | solution.py:54
  270.3 3.8 fusion.123
  274.2 3.8 convolution_add_fusion.2
  278.0 3.8 fusion.121
  281.9 3.8 convolution_subtract_fusion.3
  285.7 1.4 fusion.122
  287.1 1.7 multiply_reduce_fusion.3
  288.9 0.3 dynamic_update_slice.7
  289.7 0.3 reshape.201
  290.1 1.9 collective-permute-start.1
  292.0 131.3 %collective-permute-start.2 = (f32[5,128,8]{1,2,0:T(8,128)S(1)}, f32[5,128,8]{1,2,0:T(8,128)S(1)}, u32[]{:S(2)}, u32[]{:S(2)}) collective-permute-start(f32[5,128,8]{1,2,0:T(8,128)S(1)} %get-tuple-element.173), channel_id=1, source_target_pairs={{1,0},{2,1},{3,2},{4,3},{5,4},{6,5},{7,6},{8,7},{9,8},{10,9},{11,1... | collective-permute-start | bytes 61448 | tf_op jit(solution)/shard_map/ppermute | solution.py:19
  423.3 0.6 fusion.85
  423.9 0.3 collective-permute-done.2
  424.2 0.3 select_maximum_fusion
  424.7 0.3 add_multiply_fusion.6
  425.0 0.3 add_multiply_fusion.5
  425.3 0.3 add_multiply_fusion.4
  425.5 0.3 add_multiply_fusion.3
  425.8 0.3 add_multiply_fusion.2
  426.1 0.3 add_multiply_fusion.1
  426.4 0.3 broadcast_multiply_fusion
  426.7 0.2 slice_add_fusion.1
  427.2 0.8 copy.23
  (49 shorter events, 1.8 us)
Async XLA Ops:
  0.6 144.8 %collective-permute-start = (bf16[128,160,160]{0,2,1:T(8,128)(2,1)}, bf16[128,160,160]{0,2,1:T(8,128)(2,1)}, u32[]{:S(2)}, u32[]{:S(2)}) collective-permute-start(bf16[128,160,160]{0,2,1:T(8,128)(2,1)} %bitcast.68), channel_id=1, source_target_pairs={{16,0},{32,16},{48,32},{64,48},{80,64},{96,80},{112,96},{17,1},{33... | collective-permute-start | bytes 19660808 | tf_op jit(solution)/shard_map/ppermute | solution.py:19
  2.6 17.4 %copy-start.5 = (f32[1,1,2,128,128]{4,3,2,1,0:T(8,128)S(1)}, f32[1,1,2,128,128]{4,3,2,1,0:T(8,128)}, u32[]{:S(2)}) copy-start(f32[1,1,2,128,128]{4,3,2,1,0:T(8,128)} %param.9) | copy-start | bytes 393220
  20.9 0.6 copy-start
  22.9 137.6 %copy-start.6 = (s32[1,2,128]{2,1,0:T(2,128)S(1)}, s32[1,2,128]{2,1,0:T(2,128)}, u32[]{:S(2)}) copy-start(s32[1,2,128]{2,1,0:T(2,128)} %param.8) | copy-start | bytes 3076
  160.5 128.8 %copy-start.7 = (pred[128]{0:T(512)(128)(4,1)S(1)}, pred[128]{0:T(512)(128)(4,1)}, u32[]{:S(2)}) copy-start(pred[128]{0:T(512)(128)(4,1)} %iota_compare_fusion.2) | copy-start | bytes 388
  160.5 129.6 %copy-start.2 = (f32[1,1,2,128,128]{3,4,2,1,0:T(8,128)S(1)}, f32[1,1,2,128,128]{3,4,2,1,0:T(8,128)}, u32[]{:S(2)}) copy-start(f32[1,1,2,128,128]{3,4,2,1,0:T(8,128)} %copy.21) | copy-start | bytes 393220
  160.5 129.6 %copy-start.3 = (f32[1,128,128]{1,2,0:T(8,128)S(1)}, f32[1,128,128]{1,2,0:T(8,128)}, u32[]{:S(2)}) copy-start(f32[1,128,128]{1,2,0:T(8,128)} %reshape.202) | copy-start | bytes 196612
  289.3 135.3 %copy-start.1 = (f32[144,144]{0,1:T(8,128)S(1)}, f32[144,144]{0,1:T(8,128)}, u32[]{:S(2)}) copy-start(f32[144,144]{0,1:T(8,128)} %copy-done) | copy-start | bytes 248836
  290.1 133.8 %collective-permute-start.1 = (f32[5,128,8]{1,2,0:T(8,128)S(1)}, f32[5,128,8]{1,2,0:T(8,128)S(1)}, u32[]{:S(2)}, u32[]{:S(2)}) collective-permute-start(f32[5,128,8]{1,2,0:T(8,128)S(1)} %get-tuple-element.172), channel_id=1, source_target_pairs={{0,1},{1,2},{2,3},{3,4},{4,5},{5,6},{6,7},{7,8},{8,9},{9,10},{10,1... | collective-permute-start | bytes 61448 | tf_op jit(solution)/shard_map/ppermute | solution.py:19
  292.0 132.2 %collective-permute-start.2 = (f32[5,128,8]{1,2,0:T(8,128)S(1)}, f32[5,128,8]{1,2,0:T(8,128)S(1)}, u32[]{:S(2)}, u32[]{:S(2)}) collective-permute-start(f32[5,128,8]{1,2,0:T(8,128)S(1)} %get-tuple-element.173), channel_id=1, source_target_pairs={{1,0},{2,1},{3,2},{4,3},{5,4},{6,5},{7,6},{8,7},{9,8},{10,9},{11,1... | collective-permute-start | bytes 61448 | tf_op jit(solution)/shard_map/ppermute | solution.py:19
  424.7 2.3 copy-start.4
where the time goes:
time: 436 us; the launch traced here: 428 us
  starting transfers between devices  135 us (31%)
  waiting for transfers between devices  123 us (28%)
  matrix products  69.6 us (16%)
  other arithmetic  54.9 us (13%)
  local copies, waits for them, and re-layouts  44.1 us (10%)
    ppermute x3, starting transfers between devices, passed_along(): return lax.ppermute(block, axis, route)  135 us
    ppermute x3, waiting for transfers between devices, passed_along(): return lax.ppermute(block, axis, route)  123 us
    add x2, other arithmetic, column_transform(): spectra_all[:, :extent, :extent] + spectra_all[:, extent:, extent:]  39.3 us
    dot_general x2, matrix products, column_transform(): jnp.einsum('jm,bmk->bjk', left_table, halfway, preferred_element_type=jnp...  32.6 us
    while x3, local copies, waits for them, and re-layouts, tile_flows(): lax.fori_loop(0, count_blocks, step, jnp.zeros((2, slots), jnp.float32))  30.1 us
    sub x2, other arithmetic, window_flows(): cross_imag = real_a * imag_b - imag_a * real_b  9.85 us
    dynamic_slice x2, local copies, waits for them, and re-layouts, take(): return lax.dynamic_slice_in_dim(values, start, block_size, 0)  8.83 us
  transfers between devices with their start and end apart: 3, of which 2 were waited for; matrix products, arithmetic and copies ran while one was open for 5% of the time, Pallas kernels for 0%

commit v1 on v0

v1 whole, which is shorter than its diff:
```python
import functools

import jax
import jax.numpy as jnp
from jax import lax
from jax.experimental import pallas as pl
from jax.experimental.pallas import tpu as pltpu
from jax.sharding import PartitionSpec as P

PCOLS = 16
ITERS = 8
REACH = 3
RIM = 8

highest = lax.Precision.HIGHEST
MESH = pl.DeviceIdType.MESH


def chunk_sizes(extent):
    size = max(REACH + 1, extent // 10)
    return [size] * (extent // 2 // size) + [REACH + 1]


def build_shifted(dst, local, temp, base, low, high, row_shift, col_shift):
    extent = local.shape[0]
    row_shift = jnp.broadcast_to(row_shift, (extent, row_shift.shape[1]))
    col_shift = jnp.broadcast_to(col_shift, (extent, col_shift.shape[1]))

    def row(i, carry):
        total = None
        for k in range(-REACH, REACH + 1):
            at = base + i + k
            value = local[lax.rem(at + extent, extent)].astype(jnp.float32)
            if low > 0:
                value = value * jnp.where((at >= low) & (at < high), 1.0, 0.0)
            total = value if total is None else jnp.where(row_shift == k, value, total)
        temp[pl.ds(RIM, extent), :] = total
        temp[pl.ds(0, RIM), :] = total[extent - RIM :]
        temp[pl.ds(RIM + extent, RIM), :] = total[:RIM]
        total = None
        for k in range(-REACH, REACH + 1):
            value = temp[pl.ds(RIM + k, extent), :]
            total = value if total is None else jnp.where(col_shift == k, value, total)
        dst[i, pl.ds(RIM, extent), :] = total
        dst[i, pl.ds(0, RIM), :] = total[extent - RIM :]
        dst[i, pl.ds(RIM + extent, RIM), :] = total[:RIM]
        return carry

    lax.fori_loop(0, dst.shape[0], row, 0)


def add_lags(sums, other, shifted, start, count):
    extent, lanes = other.shape[1:]

    def row(i, totals):
        r = start + i
        value = other[r].astype(jnp.float32)
        result = []
        for a in range(3):
            for b in range(3):
                product = value * shifted[r + a, pl.ds(RIM + b - 1, extent), :]
                total = totals[3 * a + b]
                for j in range(extent // 8):
                    total = total + product[8 * j : 8 * j + 8]
                result.append(total)
        return tuple(result)

    begun = tuple(sums[k] for k in range(9))
    for k, total in enumerate(lax.fori_loop(0, count, row, begun)):
        sums[k] = total


def node_fields(lines, rows, cols):
    total = lines[0].shape[1]
    slots = total // 3
    patch_rows = slots // PCOLS
    step = cols // PCOLS
    slot = lax.broadcasted_iota(jnp.int32, (total, 2 * cols), 0)
    lane = lax.broadcasted_iota(jnp.int32, (total, 2 * cols), 1)
    part, within = slot // slots, slot % PCOLS
    home = jnp.where(
        part == 0,
        step * within,
        jnp.where(
            part == 1,
            jnp.where(within == 0, cols, -1),
            jnp.where(within == PCOLS - 1, 2 * cols - step, -1),
        ),
    )
    place = (lane == home).astype(jnp.float32)
    row_of = lax.broadcasted_iota(jnp.int32, (patch_rows, total), 1) % slots // PCOLS
    pick = row_of == lax.broadcasted_iota(jnp.int32, (patch_rows, total), 0)
    left = jnp.concatenate([jnp.where(pick, line, 0.0) for line in lines], 0)
    spots = jnp.dot(left, place, precision=highest, preferred_element_type=jnp.float32)
    spread = (
        lax.broadcasted_iota(jnp.int32, (rows, patch_rows), 0)
        == (rows // patch_rows) * lax.broadcasted_iota(jnp.int32, (rows, patch_rows), 1)
    ).astype(jnp.float32)
    return [
        jnp.dot(
            spread,
            spots[patch_rows * k : patch_rows * (k + 1)],
            precision=highest,
            preferred_element_type=jnp.float32,
        )
        for k in range(len(lines))
    ]


def relax(fields, goals, gain):
    rows = gain.shape[0]
    row = lax.broadcasted_iota(jnp.int32, gain.shape, 0)
    for _ in range(ITERS):
        following = []
        for field, goal in zip(fields, goals):
            above = jnp.where(row == 0, 0.0, pltpu.roll(field, 1, 0))
            below = jnp.where(row == rows - 1, 0.0, pltpu.roll(field, rows - 1, 0))
            left = pltpu.roll(field, 1, 1)
            right = pltpu.roll(field, field.shape[1] - 1, 1)
            following.append(0.2 * field + gain * ((above + below) + (left + right)) + goal)
        fields = following
    return fields


def kernel(
    sections, tiles,
    patch_ref, count_ref, shift_ref, prior_ref,
    flow_ref, out_ref,
    local, from_above, from_below, shifted_up, shifted_down, temp,
    far_shift, far_prior, sums, part_out, part_in, state, far_state,
    local_sem, up_send, up_recv, down_send, down_recv,
    shift_sem, part_sem, prior_sem, state_sem,
):
    sec, tile = lax.axis_index("sec"), lax.axis_index("tile")
    extent, lanes = local.shape[1:]
    half = extent // 2
    upper = half + REACH + 1
    sizes = chunk_sizes(extent)
    has_below, has_above = sec > 0, sec < sections - 1
    has_west, has_east = tile > 0, tile < tiles - 1

    def when_each(pairs):
        for have, run in pairs:
            pl.when(have)(run)

    part_out[...] = jnp.zeros_like(part_out)
    part_in[...] = jnp.zeros_like(part_in)
    state[...] = jnp.zeros_like(state)
    far_state[...] = jnp.zeros_like(far_state)
    barrier = pltpu.get_barrier_semaphore()

    def greet(where):
        return lambda: pl.semaphore_signal(
            barrier, 1, device_id=where, device_id_type=MESH
        )

    when_each(
        [
            (has_below, greet({"sec": sec - 1})),
            (has_above, greet({"sec": sec + 1})),
            (has_west, greet({"tile": tile - 1})),
            (has_east, greet({"tile": tile + 1})),
        ]
    )
    mine = pltpu.make_async_copy(patch_ref, local, local_sem)
    mine.start()
    ends = (
        jnp.where(sec == 0, 1, 0)
        + jnp.where(sec == sections - 1, 1, 0)
        + jnp.where(tile == 0, 1, 0)
        + jnp.where(tile == tiles - 1, 1, 0)
    )
    pl.semaphore_wait(barrier, 4 - ends)

    def remote(src, dst, send, recv, where):
        return pltpu.make_async_remote_copy(
            src_ref=src,
            dst_ref=dst,
            send_sem=send,
            recv_sem=recv,
            device_id=where,
            device_id_type=MESH,
        )

    shift_copy = remote(
        shift_ref, far_shift, shift_sem.at[0], shift_sem.at[1], {"sec": sec + 1}
    )
    pl.when(has_above)(shift_copy.start)
    ups, downs = [], []
    at = 0
    for c, size in enumerate(sizes):
        rows = pl.ds(at, size)
        ups.append(
            remote(patch_ref.at[rows], from_below.at[rows], up_send.at[c], up_recv.at[c], {"sec": sec + 1})
        )
        source = pl.ds((half + at) % extent, size)
        downs.append(
            remote(patch_ref.at[source], from_above.at[rows], down_send.at[c], down_recv.at[c], {"sec": sec - 1})
        )
        pl.when(has_above)(ups[c].start)
        pl.when(has_below)(downs[c].start)
        at += size
    to_east = remote(prior_ref, far_prior.at[1], prior_sem.at[0], prior_sem.at[1], {"tile": tile + 1})
    to_west = remote(prior_ref, far_prior.at[0], prior_sem.at[2], prior_sem.at[3], {"tile": tile - 1})
    pl.when(has_east)(to_east.start)
    pl.when(has_west)(to_west.start)

    sums[...] = jnp.zeros_like(sums)
    mine.wait()

    @pl.when(has_above)
    def _():
        build_shifted(
            shifted_down, local, temp, half - 1, upper, extent, -shift_ref[0:1, :], -shift_ref[1:2, :]
        )
        shift_copy.wait_send()

    @pl.when(has_below)
    def _():
        shift_copy.wait_recv()
        build_shifted(
            shifted_up, local, temp, -1, 0, extent, far_shift[0:1, :], far_shift[1:2, :]
        )

    at = 0
    for c, size in enumerate(sizes):

        @pl.when(has_below)
        def _():
            ups[c].wait_recv()
            add_lags(sums.at[0], from_below, shifted_up, at, size)

        if c == len(sizes) - 1:

            @pl.when(has_below)
            def _():
                for k in range(9):
                    part_out[k : k + 1, :] = jnp.sum(sums[0, k], axis=0, keepdims=True)

        @pl.when(has_above)
        def _():
            downs[c].wait_recv()
            add_lags(sums.at[1], from_above, shifted_down, at, size)

        at += size

    part_copy = remote(part_out, part_in, part_sem.at[0], part_sem.at[1], {"sec": sec - 1})
    pl.when(has_below)(part_copy.start)
    pl.when(has_above)(part_copy.wait_recv)

    weights = []
    for k in range(9):
        score = jnp.sum(sums[1, 8 - k], axis=0, keepdims=True) + part_in[k : k + 1, :]
        score = score / float(extent)
        weights.append(score * score)
    total = 1.0 + sum(weights)
    row_part = (weights[6] + weights[7] + weights[8] - weights[0] - weights[1] - weights[2]) / total
    col_part = (weights[2] + weights[5] + weights[8] - weights[0] - weights[3] - weights[6]) / total
    live = lax.broadcasted_iota(jnp.int32, (1, lanes), 1) < count_ref[0, 0]
    flow_a = jnp.where(live, shift_ref[0:1, :].astype(jnp.float32) + row_part, 0.0)
    flow_b = jnp.where(live, shift_ref[1:2, :].astype(jnp.float32) + col_part, 0.0)
    alive = jnp.where(live, 1.0, 0.0)
    state[0:1, :] = flow_a
    state[1:2, :] = flow_b
    state[2:3, :] = alive
    state_east = remote(state, far_state.at[1], state_sem.at[0], state_sem.at[1], {"tile": tile + 1})
    state_west = remote(state, far_state.at[0], state_sem.at[2], state_sem.at[3], {"tile": tile - 1})
    pl.when(has_east)(state_east.start)
    pl.when(has_west)(state_west.start)
    flow_ref[0:1, :] = flow_a
    flow_ref[1:2, :] = flow_b

    pl.when(has_west)(to_east.wait_recv)
    pl.when(has_east)(to_west.wait_recv)
    rows, cols = prior_ref.shape[1:]
    lane = lax.broadcasted_iota(jnp.int32, (rows, cols), 1)
    in_east = (lane < ITERS) & has_east
    in_west = (lane >= cols - ITERS) & has_west
    fields = [
        jnp.concatenate(
            [
                prior_ref[k],
                jnp.where(in_east, far_prior[0, k], jnp.where(in_west, far_prior[1, k], 0.0)),
            ],
            1,
        )
        for k in range(2)
    ]
    inside = jnp.concatenate(
        [jnp.ones((rows, cols), jnp.float32), jnp.where(in_east | in_west, 1.0, 0.0)], 1
    )
    pl.when(has_west)(state_east.wait_recv)
    pl.when(has_east)(state_west.wait_recv)
    lines = [
        jnp.concatenate([mid, far_state[0, k : k + 1, :], far_state[1, k : k + 1, :]], 1)
        for k, mid in enumerate((flow_a, flow_b, alive))
    ]
    goal_a, goal_b, weight = node_fields(lines, rows, cols)
    gain = (0.2 - 0.1 * weight) * inside
    done = relax(fields, [0.4 * goal_a, 0.4 * goal_b], gain)
    out_ref[0] = done[0][:, :cols]
    out_ref[1] = done[1][:, :cols]

    for c in range(len(sizes)):
        pl.when(has_above)(ups[c].wait_send)
        pl.when(has_below)(downs[c].wait_send)
    pl.when(has_east)(to_east.wait_send)
    pl.when(has_west)(to_west.wait_send)
    pl.when(has_below)(part_copy.wait_send)
    pl.when(has_east)(state_east.wait_send)
    pl.when(has_west)(state_west.wait_send)


def body(patches, counts, peak_shifts, mesh_prior):
    sections, tiles = lax.axis_size("sec"), lax.axis_size("tile")
    by_slot = jnp.transpose(patches[0], (1, 2, 0))
    extent, _, slots = by_slot.shape
    prior = mesh_prior[0, 0]
    chunks = len(chunk_sizes(extent))
    sent = extent // 2 + REACH + 1
    wide = (sent + 2, extent + 2 * RIM, slots)
    sems = pltpu.SemaphoreType.DMA
    vmem = pl.BlockSpec(memory_space=pltpu.VMEM)
    flows, displacement = pl.pallas_call(
        functools.partial(kernel, sections, tiles),
        in_specs=[
            pl.BlockSpec(memory_space=pl.ANY),
            pl.BlockSpec(memory_space=pltpu.SMEM),
            vmem,
            vmem,
        ],
        out_specs=[vmem, vmem],
        out_shape=[
            jax.ShapeDtypeStruct((2, slots), jnp.float32),
            jax.ShapeDtypeStruct(prior.shape, jnp.float32),
        ],
        scratch_shapes=[
            pltpu.VMEM(by_slot.shape, jnp.bfloat16),
            pltpu.VMEM((sent, extent, slots), jnp.bfloat16),
            pltpu.VMEM((sent, extent, slots), jnp.bfloat16),
            pltpu.VMEM(wide, jnp.float32),
            pltpu.VMEM(wide, jnp.float32),
            pltpu.VMEM(wide[1:], jnp.float32),
            pltpu.VMEM((2, slots), jnp.int32),
            pltpu.VMEM((2,) + prior.shape, jnp.float32),
            pltpu.VMEM((2, 9, 8, slots), jnp.float32),
            pltpu.VMEM((16, slots), jnp.float32),
            pltpu.VMEM((16, slots), jnp.float32),
            pltpu.VMEM((8, slots), jnp.float32),
            pltpu.VMEM((2, 8, slots), jnp.float32),
            sems,
            sems((chunks,)),
            sems((chunks,)),
            sems((chunks,)),
            sems((chunks,)),
            sems((2,)),
            sems((2,)),
            sems((4,)),
            sems((4,)),
        ],
        compiler_params=pltpu.CompilerParams(collective_id=0, has_side_effects=True),
    )(by_slot, counts, peak_shifts[0], prior)
    return flows[None], displacement[None, None]


def solution(mesh):
    placed = (
        P("sec", "tile", None, None),
        P("sec", "tile"),
        P("sec", None, "tile"),
        P("sec", "tile", None, None, None),
    )
    return jax.shard_map(
        body,
        mesh=mesh,
        in_specs=placed,
        out_specs=(P("sec", None, "tile"), P("sec", "tile", None, None, None)),
        check_vma=False,
    )
```

time: 436 us -> 96.6 us (0.22)
  the two profiles are of different devices: /device:TPU:1 before, /device:TPU:57 now
where the time goes in v1:
time: 96.6 us; the launch traced here: 96.4 us
  Pallas kernels  92.4 us (96%)
  local copies, waits for them, and re-layouts  2.8 us (3%)
  between operations  1.28 us (1%)
    pallas_call x1, Pallas kernels, body(): pl.pallas_call(functools.partial(kernel, sections, tiles), in_specs=[pl.B...  92.4 us
    unnamed x2, local copies, waits for them, and re-layouts  2.8 us

profile of v1, /device:TPU:57, one launch (start us, length us, event | category | flops | bytes accessed | tf_op | source)
XLA Modules:
  0.0 96.4 jit_solution(4222842229590200657)
XLA Ops:
  1.3 92.4 %shard_map.59 = (f32[2,128]{1,0:T(2,128)}, f32[2,128,128]{2,1,0:T(8,128)}) custom-call(bf16[160,160,128]{2,1,0:T(8,128)(2,1)} %bitcast.7, s32[1,1]{1,0:T(1,128)S(6)} %copy.8.count_ref, s32[2,128]{1,0:T(2,128)} %bitcast.10, f32[2,128,128]{2,1,0:T(8,128)} %bitcast.8), custom_call_target="tpu_custom_call" | custom-call | tf_op jit(solution)/shard_map/pallas_call | solution.py:324
  93.6 1.2 %copy.9 = f32[1,2,128]{2,1,0:T(2,128)} copy(f32[1,2,128]{2,1,0:T(2,128)} %bitcast.11) | data formatting | bytes 2048
  94.9 1.6 %copy.10 = f32[1,1,2,128,128]{4,3,2,1,0:T(8,128)} copy(f32[1,1,2,128,128]{4,3,2,1,0:T(8,128)} %bitcast.9) | data formatting | bytes 262144

commit v2 on v1

v2 whole, which is shorter than its diff:
```python
import functools

import jax
import jax.numpy as jnp
from jax import lax
from jax.experimental import pallas as pl
from jax.experimental.pallas import tpu as pltpu
from jax.sharding import PartitionSpec as P

PCOLS = 16
ITERS = 8
REACH = 3
RIM = 8

MESH = pl.DeviceIdType.MESH


def chunk_sizes(extent):
    half, size = extent // 2, max(6, extent // 10)
    full = half // size - 1
    up = [size] * full + [half - size * full - 4, 4]
    down = [size] * full + [half - size * full - 4, 2 * REACH]
    return up, down


def build_shifted(dst, local, temp, base, low, high, row_shift, col_shift):
    extent = local.shape[0]
    row_shift = jnp.broadcast_to(row_shift, (extent, row_shift.shape[1]))
    col_shift = jnp.broadcast_to(col_shift, (extent, col_shift.shape[1]))

    def row(i, carry):
        total = None
        for k in range(-REACH, REACH + 1):
            at = base + i + k
            value = local[lax.rem(at + extent, extent)].astype(jnp.float32)
            if low > 0:
                value = value * jnp.where((at >= low) & (at < high), 1.0, 0.0)
            total = value if total is None else jnp.where(row_shift == k, value, total)
        temp[pl.ds(RIM, extent), :] = total
        temp[pl.ds(0, RIM), :] = total[extent - RIM :]
        temp[pl.ds(RIM + extent, RIM), :] = total[:RIM]
        total = None
        for k in range(-REACH, REACH + 1):
            value = temp[pl.ds(RIM + k, extent), :]
            total = value if total is None else jnp.where(col_shift == k, value, total)
        dst[i, pl.ds(RIM, extent), :] = total
        dst[i, pl.ds(0, RIM), :] = total[extent - RIM :]
        dst[i, pl.ds(RIM + extent, RIM), :] = total[:RIM]
        return carry

    lax.fori_loop(0, dst.shape[0], row, 0)


def add_lags(sums, other, start, shifted, first, count):
    extent, lanes = other.shape[1:]

    def row(i, totals):
        value = other[start + i].astype(jnp.float32)
        result = []
        for a in range(3):
            for b in range(3):
                product = value * shifted[first + i + a, pl.ds(RIM + b - 1, extent), :]
                total = totals[3 * a + b]
                for j in range(extent // 8):
                    total = total + product[8 * j : 8 * j + 8]
                result.append(total)
        return tuple(result)

    begun = tuple(sums[k] for k in range(9))
    for k, total in enumerate(lax.fori_loop(0, count, row, begun)):
        sums[k] = total


def slot_places(extent_lanes, lanes, cols, patch_cols, homes):
    slot = lax.broadcasted_iota(jnp.int32, (2 * lanes, extent_lanes), 0)
    lane = lax.broadcasted_iota(jnp.int32, (2 * lanes, extent_lanes), 1)
    within = slot % patch_cols
    column = jnp.where(slot < lanes, within, jnp.where(within == 0, patch_cols, -1))
    return jnp.where(column == homes(lane), 1.0, 0.0).astype(jnp.bfloat16)


def by_patch_row(line, patch_rows):
    shape = (patch_rows, line.shape[1])
    slots = patch_rows * PCOLS
    of = lax.broadcasted_iota(jnp.int32, shape, 1) % slots // PCOLS
    return jnp.where(of == lax.broadcasted_iota(jnp.int32, shape, 0), line, 0.0)


def flow_lines(scores, row_shift, col_shift, live):
    weights = [score * score for score in scores]
    total = 1.0 + sum(weights)
    row_part = (weights[6] + weights[7] + weights[8] - weights[0] - weights[1] - weights[2]) / total
    col_part = (weights[2] + weights[5] + weights[8] - weights[0] - weights[3] - weights[6]) / total
    return (
        jnp.where(live > 0.0, row_shift + row_part, 0.0),
        jnp.where(live > 0.0, col_shift + col_part, 0.0),
    )


def kernel(
    sections, tiles,
    patch_ref, count_ref, shift_ref, prior_ref,
    flow_ref, out_ref,
    local, merged, from_above, from_below, shifted_up, shifted_down, shifted_rim, temp, sums,
    count, shift, far_shift, prior, far_prior, fields, goals, gain,
    info, east_info, part_up, part_down, own_up, east_up, east_down,
    local_sem, up_send, up_recv, down_send, down_recv,
    shift_sem, prior_sem, info_sem, part_sem,
):
    sec, tile = lax.axis_index("sec"), lax.axis_index("tile")
    extent, lanes = local.shape[1:]
    half = extent // 2
    rim = 2 * REACH
    low, high = half + REACH - 1, extent - REACH + 1
    up_sizes, down_sizes = chunk_sizes(extent)
    rows, cols = prior.shape[1:]
    patch_rows = lanes // PCOLS
    row_step, col_step = rows // patch_rows, cols // PCOLS
    has_below, has_above = sec > 0, sec < sections - 1
    has_west, has_east = tile > 0, tile < tiles - 1

    for buffer in (info, east_info, part_up, part_down, own_up, east_up, east_down):
        buffer[...] = jnp.zeros_like(buffer)

    barrier = pltpu.get_barrier_semaphore()
    below, above = {"sec": sec - 1}, {"sec": sec + 1}
    west, east = {"tile": tile - 1}, {"tile": tile + 1}
    below_west = {"sec": sec - 1, "tile": tile - 1}
    above_east = {"sec": sec + 1, "tile": tile + 1}
    partners = [
        (has_below, below),
        (has_above, above),
        (has_west, west),
        (has_east, east),
        (has_below & has_west, below_west),
        (has_above & has_east, above_east),
    ]

    def greet(where):
        return lambda: pl.semaphore_signal(
            barrier, 1, device_id=where, device_id_type=MESH
        )

    waits = 0
    for have, where in partners:
        pl.when(have)(greet(where))
        waits = waits + jnp.where(have, 1, 0)
    mine = [
        pltpu.make_async_copy(src, dst, local_sem.at[k])
        for k, (src, dst) in enumerate(
            ((shift_ref, shift), (count_ref, count), (patch_ref, local), (prior_ref, prior))
        )
    ]
    for copy in mine:
        copy.start()
    pl.semaphore_wait(barrier, waits)

    def remote(src, dst, sems, k, where):
        return pltpu.make_async_remote_copy(
            src_ref=src,
            dst_ref=dst,
            send_sem=sems[0].at[k],
            recv_sem=sems[1].at[k],
            device_id=where,
            device_id_type=MESH,
        )

    def remote_at(src, dst, sems, k, where):
        send, recv = sems.at[2 * k], sems.at[2 * k + 1]
        return pltpu.make_async_remote_copy(
            src_ref=src, dst_ref=dst, send_sem=send, recv_sem=recv, device_id=where, device_id_type=MESH
        )

    shift_copy = remote_at(shift_ref, far_shift, shift_sem, 0, above)
    pl.when(has_above)(shift_copy.start)
    ups, downs = [], []
    at = 0
    for c, size in enumerate(up_sizes):
        part = pl.ds(at, size)
        ups.append(remote(patch_ref.at[part], from_below.at[part], (up_send, up_recv), c, above))
        at += size
    at = 0
    for c, size in enumerate(down_sizes):
        part = pl.ds(at, size)
        source = merged if c == len(down_sizes) - 1 else patch_ref.at[pl.ds(low + at, size)]
        downs.append(remote(source, from_above.at[part], (down_send, down_recv), c, below))
        at += size
    for c in range(len(up_sizes)):
        pl.when(has_above)(ups[c].start)
        if c < len(down_sizes) - 1:
            pl.when(has_below)(downs[c].start)
    to_east = remote_at(prior_ref, far_prior.at[1], prior_sem, 0, east)
    to_west = remote_at(prior_ref, far_prior.at[0], prior_sem, 1, west)
    pl.when(has_east)(to_east.start)
    pl.when(has_west)(to_west.start)

    sums[...] = jnp.zeros_like(sums)
    for copy in mine:
        copy.wait()
    alive = jnp.where(
        lax.broadcasted_iota(jnp.int32, (1, lanes), 1) < count[0, 0], 1.0, 0.0
    )
    row_shift = shift[0:1, :].astype(jnp.float32)
    col_shift = shift[1:2, :].astype(jnp.float32)
    info[0:1, :] = row_shift
    info[1:2, :] = col_shift
    info[2:3, :] = alive

    @pl.when(has_below)
    def _():
        shift_copy.wait_recv()
        for j in range(rim):
            merged[j] = jnp.where(
                jnp.broadcast_to(far_shift[0:1, :], (extent, lanes)) <= j - REACH,
                local[half - REACH - 1 + j].astype(jnp.float32),
                local[(extent - REACH + 1 + j) % extent].astype(jnp.float32),
            ).astype(jnp.bfloat16)
        build_shifted(
            shifted_up, local, temp, -1, 0, extent, far_shift[0:1, :], far_shift[1:2, :]
        )
        downs[-1].start()

    info_copy = remote_at(info, east_info, info_sem, 0, west)
    pl.when(has_west)(info_copy.start)

    @pl.when(has_above)
    def _():
        build_shifted(
            shifted_down, local, temp, half - REACH - 2, half, extent, -shift[0:1, :], -shift[1:2, :]
        )
        for i in range(rim + 2):
            shifted_rim[i] = shifted_down[i] + shifted_down[half + 2 + i]

    pl.when(has_west)(to_east.wait_recv)
    pl.when(has_east)(to_west.wait_recv)
    pl.when(has_east)(info_copy.wait_recv)
    lane = lax.broadcasted_iota(jnp.int32, (rows, cols), 1)
    in_east = (lane < ITERS) & has_east
    in_west = (lane >= cols - ITERS) & has_west
    for k in range(2):
        fields[k, :, :cols] = prior[k]
        fields[k, :, cols:] = jnp.where(
            in_east, far_prior[0, k], jnp.where(in_west, far_prior[1, k], 0.0)
        )
        fields[2 + k] = jnp.zeros((rows, 2 * cols), jnp.float32)
    inside = jnp.concatenate(
        [jnp.ones((rows, cols), jnp.float32), jnp.where(in_east | in_west, 1.0, 0.0)], 1
    )
    at_nodes = slot_places(
        2 * cols, lanes, cols, PCOLS,
        lambda lane: jnp.where(lane % col_step == 0, lane // col_step, -2),
    )
    both_alive = jnp.concatenate([alive, east_info[2:3, :]], 1)
    spots = jnp.dot(
        by_patch_row(both_alive, patch_rows).astype(jnp.bfloat16),
        at_nodes,
        preferred_element_type=jnp.float32,
    ).astype(jnp.bfloat16)
    spread = jnp.where(
        lax.broadcasted_iota(jnp.int32, (rows, patch_rows), 0)
        == row_step * lax.broadcasted_iota(jnp.int32, (rows, patch_rows), 1),
        1.0,
        0.0,
    ).astype(jnp.bfloat16)
    weight = jnp.dot(spread, spots, preferred_element_type=jnp.float32)
    gain[...] = (0.2 - 0.1 * weight) * inside
    wide_lane = lax.broadcasted_iota(jnp.int32, weight.shape, 1)
    for k in range(2):
        goals[k] = jnp.where(wide_lane // col_step % 2 == k, 0.4 * weight, 0.0)
    row = lax.broadcasted_iota(jnp.int32, weight.shape, 0)

    def sweep(_, carry):
        for k in range(4):
            field = fields[k]
            upper = jnp.where(row == 0, 0.0, pltpu.roll(field, 1, 0))
            lower = jnp.where(row == rows - 1, 0.0, pltpu.roll(field, rows - 1, 0))
            left = pltpu.roll(field, 1, 1)
            right = pltpu.roll(field, 2 * cols - 1, 1)
            field = 0.2 * field + gain[...] * ((upper + lower) + (left + right))
            fields[k] = field + goals[k - 2] if k >= 2 else field
        return carry

    lax.fori_loop(0, ITERS, sweep, 0)
    owners = slot_places(
        2 * cols, lanes, cols, PCOLS,
        lambda lane: jnp.where(
            lane < cols,
            2 * ((lane + col_step) // (2 * col_step)),
            2 * ((lane - cols) // (2 * col_step)) + 1,
        ),
    )

    up_at = down_at = 0
    for c, (up_size, down_size) in enumerate(zip(up_sizes, down_sizes, strict=True)):
        final = c == len(up_sizes) - 1

        @pl.when(has_below)
        def _():
            ups[c].wait_recv()
            add_lags(sums.at[0], from_below, up_at, shifted_up, up_at, up_size)

        if final:

            @pl.when(has_below)
            def _():
                for k in range(9):
                    part_up[k : k + 1, :] = jnp.sum(sums[0, k], axis=0, keepdims=True)

            up_part = remote_at(part_up, own_up, part_sem, 0, below)
            up_part_west = remote_at(part_up, east_up, part_sem, 1, below_west)
            pl.when(has_below)(up_part.start)
            pl.when(has_below & has_west)(up_part_west.start)

        @pl.when(has_above)
        def _():
            downs[c].wait_recv()
            if final:
                add_lags(sums.at[1], from_above, down_at, shifted_rim, 0, down_size)
            else:
                add_lags(sums.at[1], from_above, down_at, shifted_down, down_at + rim, down_size)

        up_at += up_size
        down_at += down_size

    for k in range(9):
        part_down[k : k + 1, :] = jnp.sum(sums[1, 8 - k], axis=0, keepdims=True)
    down_part = remote_at(part_down, east_down, part_sem, 2, west)
    pl.when(has_west)(down_part.start)

    pl.when(has_above)(up_part.wait_recv)
    scale = float(extent)
    flow_a, flow_b = flow_lines(
        [(part_down[k : k + 1, :] + own_up[k : k + 1, :]) / scale for k in range(9)],
        row_shift,
        col_shift,
        alive,
    )
    flow_ref[0:1, :] = flow_a
    flow_ref[1:2, :] = flow_b
    pl.when(has_east)(down_part.wait_recv)
    pl.when(has_above & has_east)(up_part_west.wait_recv)
    east_a, east_b = flow_lines(
        [(east_down[k : k + 1, :] + east_up[k : k + 1, :]) / scale for k in range(9)],
        east_info[0:1, :],
        east_info[1:2, :],
        east_info[2:3, :],
    )
    left = jnp.concatenate(
        [
            by_patch_row(jnp.concatenate([flow_a, east_a], 1), patch_rows),
            by_patch_row(jnp.concatenate([flow_b, east_b], 1), patch_rows),
        ],
        0,
    )
    first = left.astype(jnp.bfloat16)
    rest = left - first.astype(jnp.float32)
    second = rest.astype(jnp.bfloat16)
    third = (rest - second.astype(jnp.float32)).astype(jnp.bfloat16)
    values = sum(
        jnp.dot(piece, owners, preferred_element_type=jnp.float32)
        for piece in (first, second, third)
    )
    strip = row_step // 2
    for m in range(rows // strip):
        owner = (m + 1) // 2
        part = pl.ds(m * strip, strip)
        for k in range(2):
            result = fields[k, part, :cols]
            if owner < patch_rows:
                value = values[k * patch_rows + owner : k * patch_rows + owner + 1]
                result = (
                    result
                    + fields[2, part, :cols] * value[:, :cols]
                    + fields[3, part, :cols] * value[:, cols:]
                )
            out_ref[k, part, :] = result

    pl.when(has_above)(shift_copy.wait_send)
    for copy in ups:
        pl.when(has_above)(copy.wait_send)
    for copy in downs:
        pl.when(has_below)(copy.wait_send)
    pl.when(has_east)(to_east.wait_send)
    pl.when(has_west)(to_west.wait_send)
    pl.when(has_west)(info_copy.wait_send)
    pl.when(has_below)(up_part.wait_send)
    pl.when(has_below & has_west)(up_part_west.wait_send)
    pl.when(has_west)(down_part.wait_send)


def body(patches, counts, peak_shifts, mesh_prior):
    sections, tiles = lax.axis_size("sec"), lax.axis_size("tile")
    by_slot = jnp.transpose(patches[0], (1, 2, 0))
    extent, _, slots = by_slot.shape
    prior = mesh_prior[0, 0]
    rows, cols = prior.shape[1:]
    half, rim = extent // 2, 2 * REACH
    up_sizes, down_sizes = chunk_sizes(extent)
    padded = extent + 2 * RIM
    sems = pltpu.SemaphoreType.DMA
    vmem = pl.BlockSpec(memory_space=pltpu.VMEM)
    f32, bf16 = jnp.float32, jnp.bfloat16
    flows, displacement = pl.pallas_call(
        functools.partial(kernel, sections, tiles),
        in_specs=[pl.BlockSpec(memory_space=pl.ANY)] * 4,
        out_specs=[vmem, vmem],
        out_shape=[
            jax.ShapeDtypeStruct((2, slots), f32),
            jax.ShapeDtypeStruct(prior.shape, f32),
        ],
        scratch_shapes=[
            pltpu.VMEM(by_slot.shape, bf16),
            pltpu.VMEM((rim, extent, slots), bf16),
            pltpu.VMEM((sum(down_sizes), extent, slots), bf16),
            pltpu.VMEM((sum(up_sizes), extent, slots), bf16),
            pltpu.VMEM((half + 2, padded, slots), f32),
            pltpu.VMEM((half + 4 + rim, padded, slots), f32),
            pltpu.VMEM((rim + 2, padded, slots), f32),
            pltpu.VMEM((padded, slots), f32),
            pltpu.VMEM((2, 9, 8, slots), f32),
            pltpu.SMEM((1, 1), jnp.int32),
            pltpu.VMEM((2, slots), jnp.int32),
            pltpu.VMEM((2, slots), jnp.int32),
            pltpu.VMEM(prior.shape, f32),
            pltpu.VMEM((2,) + prior.shape, f32),
            pltpu.VMEM((4, rows, 2 * cols), f32),
            pltpu.VMEM((2, rows, 2 * cols), f32),
            pltpu.VMEM((rows, 2 * cols), f32),
            pltpu.VMEM((8, slots), f32),
            pltpu.VMEM((8, slots), f32),
            pltpu.VMEM((16, slots), f32),
            pltpu.VMEM((16, slots), f32),
            pltpu.VMEM((16, slots), f32),
            pltpu.VMEM((16, slots), f32),
            pltpu.VMEM((16, slots), f32),
            sems((4,)),
            sems((len(up_sizes),)),
            sems((len(up_sizes),)),
            sems((len(down_sizes),)),
            sems((len(down_sizes),)),
            sems((2,)),
            sems((4,)),
            sems((2,)),
            sems((6,)),
        ],
        compiler_params=pltpu.CompilerParams(collective_id=0, has_side_effects=True),
    )(by_slot, counts, peak_shifts[0], prior)
    return flows[None], displacement[None, None]


def solution(mesh):
    placed = (
        P("sec", "tile", None, None),
        P("sec", "tile"),
        P("sec", None, "tile"),
        P("sec", "tile", None, None, None),
    )
    return jax.shard_map(
        body,
        mesh=mesh,
        in_specs=placed,
        out_specs=(P("sec", None, "tile"), P("sec", "tile", None, None, None)),
        check_vma=False,
    )
```

time: 96.6 us -> 96 us (level)
  the two profiles are of different devices: /device:TPU:57 before, /device:TPU:83 now
where the time goes in v2:
time: 96 us; the launch traced here: 95.8 us
  Pallas kernels  91.8 us (96%)
  local copies, waits for them, and re-layouts  2.8 us (3%)
  between operations  1.28 us (1%)
    pallas_call x1, Pallas kernels, body(): pl.pallas_call(functools.partial(kernel, sections, tiles), in_specs=[pl.B...  91.8 us
    unnamed x2, local copies, waits for them, and re-layouts  2.8 us

profile of v2, /device:TPU:83, one launch (start us, length us, event | category | flops | bytes accessed | tf_op | source)
XLA Modules:
  0.0 95.8 jit_solution(5546829156656533381)
XLA Ops:
  1.3 91.8 %shard_map.59 = (f32[2,128]{1,0:T(2,128)}, f32[2,128,128]{2,1,0:T(8,128)}) custom-call(bf16[160,160,128]{2,1,0:T(8,128)(2,1)} %bitcast.7, s32[1,1]{1,0:T(1,128)S(6)} %copy.8.count_ref, s32[2,128]{1,0:T(2,128)} %bitcast.10, f32[2,128,128]{2,1,0:T(8,128)} %bitcast.8), custom_call_target="tpu_custom_call" | custom-call | tf_op jit(solution)/shard_map/pallas_call | solution.py:403
  93.0 1.2 %copy.9 = f32[1,2,128]{2,1,0:T(2,128)} copy(f32[1,2,128]{2,1,0:T(2,128)} %bitcast.11) | data formatting | bytes 2048
  94.3 1.6 %copy.10 = f32[1,1,2,128,128]{4,3,2,1,0:T(8,128)} copy(f32[1,1,2,128,128]{4,3,2,1,0:T(8,128)} %bitcast.9) | data formatting | bytes 262144

commit v3 on v2

--- a/solution.py
+++ b/solution.py
@@ -102,10 +102,10 @@
     patch_ref, count_ref, shift_ref, prior_ref,
     flow_ref, out_ref,
     local, merged, from_above, from_below, shifted_up, shifted_down, shifted_rim, temp, sums,
-    count, shift, far_shift, prior, far_prior, fields, goals, gain,
+    count, shift, far_shift, prior, rims, far_rims, fields, goals, gain,
     info, east_info, part_up, part_down, own_up, east_up, east_down,
     local_sem, up_send, up_recv, down_send, down_recv,
-    shift_sem, prior_sem, info_sem, part_sem,
+    shift_sem, rim_sem, info_sem, part_sem,
 ):
     sec, tile = lax.axis_index("sec"), lax.axis_index("tile")
     extent, lanes = local.shape[1:]
@@ -119,6 +119,7 @@
     has_below, has_above = sec > 0, sec < sections - 1
     has_west, has_east = tile > 0, tile < tiles - 1
 
+    far_rims[...] = jnp.zeros_like(far_rims)
     for buffer in (info, east_info, part_up, part_down, own_up, east_up, east_down):
         buffer[...] = jnp.zeros_like(buffer)
 
@@ -126,14 +127,11 @@
     below, above = {"sec": sec - 1}, {"sec": sec + 1}
     west, east = {"tile": tile - 1}, {"tile": tile + 1}
     below_west = {"sec": sec - 1, "tile": tile - 1}
-    above_east = {"sec": sec + 1, "tile": tile + 1}
     partners = [
         (has_below, below),
         (has_above, above),
         (has_west, west),
         (has_east, east),
-        (has_below & has_west, below_west),
-        (has_above & has_east, above_east),
     ]
 
     def greet(where):
@@ -148,11 +146,26 @@
     mine = [
         pltpu.make_async_copy(src, dst, local_sem.at[k])
         for k, (src, dst) in enumerate(
-            ((shift_ref, shift), (count_ref, count), (patch_ref, local), (prior_ref, prior))
+            ((shift_ref, shift), (count_ref, count), (prior_ref, prior), (patch_ref, local))
         )
     ]
     for copy in mine:
         copy.start()
+    mine[0].wait()
+    mine[1].wait()
+    alive = jnp.where(
+        lax.broadcasted_iota(jnp.int32, (1, lanes), 1) < count[0, 0], 1.0, 0.0
+    )
+    row_shift = shift[0:1, :].astype(jnp.float32)
+    col_shift = shift[1:2, :].astype(jnp.float32)
+    info[0:1, :] = row_shift
+    info[1:2, :] = col_shift
+    info[2:3, :] = alive
+    mine[2].wait()
+    for k in range(2):
+        turned = jnp.transpose(prior[k])
+        rims[0, k] = turned[:ITERS]
+        rims[1, k] = turned[cols - ITERS :]
     pl.semaphore_wait(barrier, waits)
 
     def remote(src, dst, sems, k, where):
@@ -173,6 +186,12 @@
 
     shift_copy = remote_at(shift_ref, far_shift, shift_sem, 0, above)
     pl.when(has_above)(shift_copy.start)
+    info_copy = remote_at(info, east_info, info_sem, 0, west)
+    pl.when(has_west)(info_copy.start)
+    to_east = remote_at(rims.at[1], far_rims.at[1], rim_sem, 0, east)
+    to_west = remote_at(rims.at[0], far_rims.at[0], rim_sem, 1, west)
+    pl.when(has_east)(to_east.start)
+    pl.when(has_west)(to_west.start)
     ups, downs = [], []
     at = 0
     for c, size in enumerate(up_sizes):
@@ -189,22 +208,8 @@
         pl.when(has_above)(ups[c].start)
         if c < len(down_sizes) - 1:
             pl.when(has_below)(downs[c].start)
-    to_east = remote_at(prior_ref, far_prior.at[1], prior_sem, 0, east)
-    to_west = remote_at(prior_ref, far_prior.at[0], prior_sem, 1, west)
-    pl.when(has_east)(to_east.start)
-    pl.when(has_west)(to_west.start)
-
     sums[...] = jnp.zeros_like(sums)
-    for copy in mine:
-        copy.wait()
-    alive = jnp.where(
-        lax.broadcasted_iota(jnp.int32, (1, lanes), 1) < count[0, 0], 1.0, 0.0
-    )
-    row_shift = shift[0:1, :].astype(jnp.float32)
-    col_shift = shift[1:2, :].astype(jnp.float32)
-    info[0:1, :] = row_shift
-    info[1:2, :] = col_shift
-    info[2:3, :] = alive
+    mine[3].wait()
 
     @pl.when(has_below)
     def _():
@@ -220,9 +225,6 @@
         )
         downs[-1].start()
 
-    info_copy = remote_at(info, east_info, info_sem, 0, west)
-    pl.when(has_west)(info_copy.start)
-
     @pl.when(has_above)
     def _():
         build_shifted(
@@ -239,8 +241,9 @@
     in_west = (lane >= cols - ITERS) & has_west
     for k in range(2):
         fields[k, :, :cols] = prior[k]
-        fields[k, :, cols:] = jnp.where(
-            in_east, far_prior[0, k], jnp.where(in_west, far_prior[1, k], 0.0)
+        between = jnp.zeros((cols - 2 * ITERS, rows), jnp.float32)
+        fields[k, :, cols:] = jnp.transpose(
+            jnp.concatenate([far_rims[0, k], between, far_rims[1, k]], 0)
         )
         fields[2 + k] = jnp.zeros((rows, 2 * cols), jnp.float32)
     inside = jnp.concatenate(
@@ -402,7 +405,7 @@
     f32, bf16 = jnp.float32, jnp.bfloat16
     flows, displacement = pl.pallas_call(
         functools.partial(kernel, sections, tiles),
-        in_specs=[pl.BlockSpec(memory_space=pl.ANY)] * 4,
+        in_specs=[pl.BlockSpec(memory_space=pltpu.HBM)] * 4,
         out_specs=[vmem, vmem],
         out_shape=[
             jax.ShapeDtypeStruct((2, slots), f32),
@@ -422,7 +425,8 @@
             pltpu.VMEM((2, slots), jnp.int32),
             pltpu.VMEM((2, slots), jnp.int32),
             pltpu.VMEM(prior.shape, f32),
-            pltpu.VMEM((2,) + prior.shape, f32),
+            pltpu.VMEM((2, 2, ITERS, rows), f32),
+            pltpu.VMEM((2, 2, ITERS, rows), f32),
             pltpu.VMEM((4, rows, 2 * cols), f32),
             pltpu.VMEM((2, rows, 2 * cols), f32),
             pltpu.VMEM((rows, 2 * cols), f32),

time: 96 us -> 87.8 us (0.915)
  the two profiles are of different devices: /device:TPU:83 before, /device:TPU:1 now
where the time goes in v3:
time: 87.8 us; the launch traced here: 86.1 us
  Pallas kernels  82 us (93%)
  local copies, waits for them, and re-layouts  2.8 us (3%)
  between operations  1.28 us (1%)
    pallas_call x1, Pallas kernels, body(): pl.pallas_call(functools.partial(kernel, sections, tiles), in_specs=[pl.B...  82 us
    unnamed x2, local copies, waits for them, and re-layouts  2.8 us

profile of v3, /device:TPU:1, one launch (start us, length us, event | category | flops | bytes accessed | tf_op | source)
XLA Modules:
  0.0 86.1 jit_solution(8293316881841502163)
XLA Ops:
  1.3 82.0 %shard_map.59 = (f32[2,128]{1,0:T(2,128)}, f32[2,128,128]{2,1,0:T(8,128)}) custom-call(bf16[160,160,128]{2,1,0:T(8,128)(2,1)} %bitcast.7, s32[1,1]{1,0:T(1,128)S(6)} %copy.8.count_ref, s32[2,128]{1,0:T(2,128)} %bitcast.10, f32[2,128,128]{2,1,0:T(8,128)} %bitcast.8), custom_call_target="tpu_custom_call" | custom-call | tf_op jit(solution)/shard_map/pallas_call | solution.py:406
  83.3 1.2 %copy.9 = f32[1,2,128]{2,1,0:T(2,128)} copy(f32[1,2,128]{2,1,0:T(2,128)} %bitcast.11) | data formatting | bytes 2048
  84.5 1.6 %copy.10 = f32[1,1,2,128,128]{4,3,2,1,0:T(8,128)} copy(f32[1,1,2,128,128]{4,3,2,1,0:T(8,128)} %bitcast.9) | data formatting | bytes 262144

commit v4 on v3

--- a/solution.py
+++ b/solution.py
@@ -15,11 +15,16 @@
 MESH = pl.DeviceIdType.MESH
 
 
+def rows_up(extent):
+    return extent // 2 - 1
+
+
 def chunk_sizes(extent):
-    half, size = extent // 2, max(6, extent // 10)
-    full = half // size - 1
-    up = [size] * full + [half - size * full - 4, 4]
-    down = [size] * full + [half - size * full - 4, 2 * REACH]
+    size = max(6, extent // 10)
+    full = extent // 2 // size - 1
+    sent = rows_up(extent)
+    up = [size] * full + [sent - size * full - 4, 4]
+    down = [size] * full + [extent - sent - REACH - 1 - size * full, 2 * REACH]
     return up, down
 
 
@@ -100,7 +105,7 @@
 def kernel(
     sections, tiles,
     patch_ref, count_ref, shift_ref, prior_ref,
-    flow_ref, out_ref,
+    line_ref, base_ref, owner_ref,
     local, merged, from_above, from_below, shifted_up, shifted_down, shifted_rim, temp, sums,
     count, shift, far_shift, prior, rims, far_rims, fields, goals, gain,
     info, east_info, part_up, part_down, own_up, east_up, east_down,
@@ -109,17 +114,19 @@
 ):
     sec, tile = lax.axis_index("sec"), lax.axis_index("tile")
     extent, lanes = local.shape[1:]
-    half = extent // 2
+    sent = rows_up(extent)
     rim = 2 * REACH
-    low, high = half + REACH - 1, extent - REACH + 1
+    low = sent + REACH - 1
     up_sizes, down_sizes = chunk_sizes(extent)
     rows, cols = prior.shape[1:]
     patch_rows = lanes // PCOLS
     row_step, col_step = rows // patch_rows, cols // PCOLS
     has_below, has_above = sec > 0, sec < sections - 1
     has_west, has_east = tile > 0, tile < tiles - 1
+    even = lax.rem(tile, 2) == 0
 
     far_rims[...] = jnp.zeros_like(far_rims)
+    line_ref[...] = jnp.zeros_like(line_ref)
     for buffer in (info, east_info, part_up, part_down, own_up, east_up, east_down):
         buffer[...] = jnp.zeros_like(buffer)
 
@@ -217,21 +224,21 @@
         for j in range(rim):
             merged[j] = jnp.where(
                 jnp.broadcast_to(far_shift[0:1, :], (extent, lanes)) <= j - REACH,
-                local[half - REACH - 1 + j].astype(jnp.float32),
+                local[sent - REACH - 1 + j].astype(jnp.float32),
                 local[(extent - REACH + 1 + j) % extent].astype(jnp.float32),
             ).astype(jnp.bfloat16)
         build_shifted(
             shifted_up, local, temp, -1, 0, extent, far_shift[0:1, :], far_shift[1:2, :]
         )
-        downs[-1].start()
+        pl.when(even)(downs[-1].start)
 
     @pl.when(has_above)
     def _():
         build_shifted(
-            shifted_down, local, temp, half - REACH - 2, half, extent, -shift[0:1, :], -shift[1:2, :]
+            shifted_down, local, temp, sent - REACH - 2, sent, extent, -shift[0:1, :], -shift[1:2, :]
         )
         for i in range(rim + 2):
-            shifted_rim[i] = shifted_down[i] + shifted_down[half + 2 + i]
+            shifted_rim[i] = shifted_down[i] + shifted_down[extent - sent + 2 + i]
 
     pl.when(has_west)(to_east.wait_recv)
     pl.when(has_east)(to_west.wait_recv)
@@ -284,7 +291,9 @@
         return carry
 
     lax.fori_loop(0, ITERS, sweep, 0)
-    owners = slot_places(
+    for k in range(4):
+        base_ref[k] = fields[k, :, :cols]
+    owner_ref[...] = slot_places(
         2 * cols, lanes, cols, PCOLS,
         lambda lane: jnp.where(
             lane < cols,
@@ -322,6 +331,8 @@
             else:
                 add_lags(sums.at[1], from_above, down_at, shifted_down, down_at + rim, down_size)
 
+        if c == len(up_sizes) - 2:
+            pl.when(has_below & ~even)(downs[-1].start)
         up_at += up_size
         down_at += down_size
 
@@ -338,8 +349,8 @@
         col_shift,
         alive,
     )
-    flow_ref[0:1, :] = flow_a
-    flow_ref[1:2, :] = flow_b
+    line_ref[0:1, :] = flow_a
+    line_ref[1:2, :] = flow_b
     pl.when(has_east)(down_part.wait_recv)
     pl.when(has_above & has_east)(up_part_west.wait_recv)
     east_a, east_b = flow_lines(
@@ -348,35 +359,8 @@
         east_info[1:2, :],
         east_info[2:3, :],
     )
-    left = jnp.concatenate(
-        [
-            by_patch_row(jnp.concatenate([flow_a, east_a], 1), patch_rows),
-            by_patch_row(jnp.concatenate([flow_b, east_b], 1), patch_rows),
-        ],
-        0,
-    )
-    first = left.astype(jnp.bfloat16)
-    rest = left - first.astype(jnp.float32)
-    second = rest.astype(jnp.bfloat16)
-    third = (rest - second.astype(jnp.float32)).astype(jnp.bfloat16)
-    values = sum(
-        jnp.dot(piece, owners, preferred_element_type=jnp.float32)
-        for piece in (first, second, third)
-    )
-    strip = row_step // 2
-    for m in range(rows // strip):
-        owner = (m + 1) // 2
-        part = pl.ds(m * strip, strip)
-        for k in range(2):
-            result = fields[k, part, :cols]
-            if owner < patch_rows:
-                value = values[k * patch_rows + owner : k * patch_rows + owner + 1]
-                result = (
-                    result
-                    + fields[2, part, :cols] * value[:, :cols]
-                    + fields[3, part, :cols] * value[:, cols:]
-                )
-            out_ref[k, part, :] = result
+    line_ref[2:3, :] = east_a
+    line_ref[3:4, :] = east_b
 
     pl.when(has_above)(shift_copy.wait_send)
     for copy in ups:
@@ -391,33 +375,73 @@
     pl.when(has_west)(down_part.wait_send)
 
 
+def finish_kernel(line_ref, base_ref, owner_ref, flow_ref, out_ref):
+    rows, cols = base_ref.shape[1:]
+    patch_rows = line_ref.shape[1] // PCOLS
+    step = rows // patch_rows
+    flow_ref[...] = line_ref[0:2, :]
+    left = jnp.concatenate(
+        [
+            by_patch_row(
+                jnp.concatenate([line_ref[k : k + 1, :], line_ref[k + 2 : k + 3, :]], 1), patch_rows
+            )
+            for k in range(2)
+        ],
+        0,
+    )
+    first = left.astype(jnp.bfloat16)
+    rest = left - first.astype(jnp.float32)
+    second = rest.astype(jnp.bfloat16)
+    third = (rest - second.astype(jnp.float32)).astype(jnp.bfloat16)
+    parts = jnp.dot(
+        jnp.concatenate([first, second, third], 0), owner_ref[...], preferred_element_type=jnp.float32
+    )
+    size = 2 * patch_rows
+    values = parts[:size] + parts[size : 2 * size] + parts[2 * size :]
+    strip = step // 2
+    for m in range(rows // strip):
+        owner = (m + 1) // 2
+        part = pl.ds(m * strip, strip)
+        for k in range(2):
+            result = base_ref[k, part, :]
+            if owner < patch_rows:
+                value = values[k * patch_rows + owner : k * patch_rows + owner + 1]
+                result = (
+                    result
+                    + base_ref[2, part, :] * value[:, :cols]
+                    + base_ref[3, part, :] * value[:, cols:]
+                )
+            out_ref[k, part, :] = result
+
+
 def body(patches, counts, peak_shifts, mesh_prior):
     sections, tiles = lax.axis_size("sec"), lax.axis_size("tile")
     by_slot = jnp.transpose(patches[0], (1, 2, 0))
     extent, _, slots = by_slot.shape
     prior = mesh_prior[0, 0]
     rows, cols = prior.shape[1:]
-    half, rim = extent // 2, 2 * REACH
+    sent, rim = rows_up(extent), 2 * REACH
     up_sizes, down_sizes = chunk_sizes(extent)
     padded = extent + 2 * RIM
     sems = pltpu.SemaphoreType.DMA
     vmem = pl.BlockSpec(memory_space=pltpu.VMEM)
     f32, bf16 = jnp.float32, jnp.bfloat16
-    flows, displacement = pl.pallas_call(
+    lines, base, owners = pl.pallas_call(
         functools.partial(kernel, sections, tiles),
         in_specs=[pl.BlockSpec(memory_space=pltpu.HBM)] * 4,
-        out_specs=[vmem, vmem],
+        out_specs=[vmem, vmem, vmem],
         out_shape=[
-            jax.ShapeDtypeStruct((2, slots), f32),
-            jax.ShapeDtypeStruct(prior.shape, f32),
+            pltpu.VMEM((8, slots), f32),
+            pltpu.VMEM((4, rows, cols), f32),
+            pltpu.VMEM((2 * slots, 2 * cols), bf16),
         ],
         scratch_shapes=[
             pltpu.VMEM(by_slot.shape, bf16),
             pltpu.VMEM((rim, extent, slots), bf16),
             pltpu.VMEM((sum(down_sizes), extent, slots), bf16),
             pltpu.VMEM((sum(up_sizes), extent, slots), bf16),
-            pltpu.VMEM((half + 2, padded, slots), f32),
-            pltpu.VMEM((half + 4 + rim, padded, slots), f32),
+            pltpu.VMEM((sent + 2, padded, slots), f32),
+            pltpu.VMEM((extent - sent + 4 + rim, padded, slots), f32),
             pltpu.VMEM((rim + 2, padded, slots), f32),
             pltpu.VMEM((padded, slots), f32),
             pltpu.VMEM((2, 9, 8, slots), f32),
@@ -449,6 +473,15 @@
         ],
         compiler_params=pltpu.CompilerParams(collective_id=0, has_side_effects=True),
     )(by_slot, counts, peak_shifts[0], prior)
+    flows, displacement = pl.pallas_call(
+        finish_kernel,
+        in_specs=[vmem, vmem, vmem],
+        out_specs=[vmem, vmem],
+        out_shape=[
+            jax.ShapeDtypeStruct((2, slots), f32),
+            jax.ShapeDtypeStruct(prior.shape, f32),
+        ],
+    )(*[pltpu.with_memory_space_constraint(x, pltpu.VMEM) for x in (lines, base, owners)])
     return flows[None], displacement[None, None]
 
 

time: 87.8 us -> 84.1 us (0.958)
  local copies, waits for them, and re-layouts: 2.8 us -> 0 us
    unnamed x2 -> x0, local copies, waits for them, and re-layouts: 2.8 us -> none
    pallas_call x1, Pallas kernels: 82 us -> 80.9 us  [body(): pl.pallas_call(functools.partial(kernel, sections, tiles), in_specs=[pl.B...]
where the time goes in v4:
time: 84.1 us; the launch traced here: 83.1 us
  Pallas kernels  81.8 us (97%)
  between operations  1.28 us (2%)
    pallas_call x1, Pallas kernels, body(): pl.pallas_call(functools.partial(kernel, sections, tiles), in_specs=[pl.B...  80.9 us

profile of v4, /device:TPU:1, one launch (start us, length us, event | category | flops | bytes accessed | tf_op | source)
XLA Modules:
  0.0 83.1 jit_solution(15627438802899611260)
XLA Ops:
  1.3 80.9 %shard_map.59 = (f32[8,128]{1,0:T(8,128)S(1)}, f32[4,128,128]{2,1,0:T(8,128)S(1)}, bf16[256,256]{1,0:T(8,128)(2,1)S(1)}) custom-call(bf16[160,160,128]{2,1,0:T(8,128)(2,1)} %bitcast.7, s32[1,1]{1,0:T(1,128)S(6)} %copy.6.count_ref, s32[2,128]{1,0:T(2,128)} %bitcast.9, f32[2,128,128]{2,1,0:T(8,128)} %bitcast.8), custom_call_target="tpu_custom_call" | custom-call | tf_op jit(solution)/shard_map/pallas_call | solution.py:429
  82.2 0.8 %shard_map.60 = (f32[2,128]{1,0:T(2,128)}, f32[2,128,128]{2,1,0:T(8,128)}) custom-call(f32[8,128]{1,0:T(8,128)S(1)} %get-tuple-element.7.line_ref, f32[4,128,128]{2,1,0:T(8,128)S(1)} %get-tuple-element.8.base_ref, bf16[256,256]{1,0:T(8,128)(2,1)S(1)} %get-tuple-element.9.owner_ref), custom_call_target="tpu_custom_call" | custom-call | tf_op jit(solution)/shard_map/pallas_call | solution.py:476

commit v5 on v4

--- a/solution.py
+++ b/solution.py
@@ -16,7 +16,7 @@
 
 
 def rows_up(extent):
-    return extent // 2 - 1
+    return extent // 2 + 1
 
 
 def chunk_sizes(extent):
@@ -110,7 +110,7 @@
     count, shift, far_shift, prior, rims, far_rims, fields, goals, gain,
     info, east_info, part_up, part_down, own_up, east_up, east_down,
     local_sem, up_send, up_recv, down_send, down_recv,
-    shift_sem, rim_sem, info_sem, part_sem,
+    shift_sem, rim_sem, info_sem, part_sem, relay_sem,
 ):
     sec, tile = lax.axis_index("sec"), lax.axis_index("tile")
     extent, lanes = local.shape[1:]
@@ -124,6 +124,10 @@
     has_below, has_above = sec > 0, sec < sections - 1
     has_west, has_east = tile > 0, tile < tiles - 1
     even = lax.rem(tile, 2) == 0
+    middle, relay = sections // 2, len(up_sizes) - 2
+    is_low, is_high = sec == middle - 1, sec == middle
+    is_first, is_last = sec == 0, sec == sections - 1
+    late_up, late_down = ~even & ~is_low, ~even & ~is_high
 
     far_rims[...] = jnp.zeros_like(far_rims)
     line_ref[...] = jnp.zeros_like(line_ref)
@@ -139,17 +143,19 @@
         (has_above, above),
         (has_west, west),
         (has_east, east),
+        (is_first, {"sec": middle}),
+        (is_last, {"sec": middle - 1}),
     ]
+    greeted = [has_below, has_above, has_west, has_east, is_low, is_high]
 
     def greet(where):
         return lambda: pl.semaphore_signal(
             barrier, 1, device_id=where, device_id_type=MESH
         )
 
-    waits = 0
     for have, where in partners:
         pl.when(have)(greet(where))
-        waits = waits + jnp.where(have, 1, 0)
+    waits = sum(jnp.where(have, 1, 0) for have in greeted)
     mine = [
         pltpu.make_async_copy(src, dst, local_sem.at[k])
         for k, (src, dst) in enumerate(
@@ -211,10 +217,37 @@
         source = merged if c == len(down_sizes) - 1 else patch_ref.at[pl.ds(low + at, size)]
         downs.append(remote(source, from_above.at[part], (down_send, down_recv), c, below))
         at += size
+    held_up, held_down = pl.ds(0, up_sizes[relay]), pl.ds(0, down_sizes[relay])
+    up_source = pl.ds(sum(up_sizes[:relay]), up_sizes[relay])
+    down_offset = sum(down_sizes[:relay])
+    up_leg = remote_at(
+        patch_ref.at[up_source], from_above.at[held_up], relay_sem, 0, {"sec": sections - 1}
+    )
+    down_leg = remote_at(
+        patch_ref.at[pl.ds(low + down_offset, down_sizes[relay])],
+        from_below.at[held_down],
+        relay_sem,
+        1,
+        {"sec": 0},
+    )
+    up_on = remote(
+        from_above.at[held_up], from_below.at[up_source], (up_send, up_recv), relay, {"sec": middle}
+    )
+    down_on = remote(
+        from_below.at[held_down],
+        from_above.at[pl.ds(down_offset, down_sizes[relay])],
+        (down_send, down_recv),
+        relay,
+        {"sec": middle - 1},
+    )
+    pl.when(is_low)(up_leg.start)
+    pl.when(is_high)(down_leg.start)
     for c in range(len(up_sizes)):
-        pl.when(has_above)(ups[c].start)
-        if c < len(down_sizes) - 1:
-            pl.when(has_below)(downs[c].start)
+        last = c == len(up_sizes) - 1
+        sends_up = has_above & ~late_up if last else has_above
+        pl.when(sends_up & ~is_low if c == relay else sends_up)(ups[c].start)
+        if not last:
+            pl.when(has_below & ~is_high if c == relay else has_below)(downs[c].start)
     sums[...] = jnp.zeros_like(sums)
     mine[3].wait()
 
@@ -230,7 +263,7 @@
         build_shifted(
             shifted_up, local, temp, -1, 0, extent, far_shift[0:1, :], far_shift[1:2, :]
         )
-        pl.when(even)(downs[-1].start)
+        pl.when(~late_down)(downs[-1].start)
 
     @pl.when(has_above)
     def _():
@@ -302,6 +335,16 @@
         ),
     )
 
+    @pl.when(is_first)
+    def _():
+        down_leg.wait_recv()
+        down_on.start()
+
+    @pl.when(is_last)
+    def _():
+        up_leg.wait_recv()
+        up_on.start()
+
     up_at = down_at = 0
     for c, (up_size, down_size) in enumerate(zip(up_sizes, down_sizes, strict=True)):
         final = c == len(up_sizes) - 1
@@ -311,6 +354,8 @@
             ups[c].wait_recv()
             add_lags(sums.at[0], from_below, up_at, shifted_up, up_at, up_size)
 
+        if c == len(up_sizes) - 2:
+            pl.when(has_above & late_up)(ups[-1].start)
         if final:
 
             @pl.when(has_below)
@@ -322,6 +367,9 @@
             up_part_west = remote_at(part_up, east_up, part_sem, 1, below_west)
             pl.when(has_below)(up_part.start)
             pl.when(has_below & has_west)(up_part_west.start)
+
+        if c == relay:
+            pl.when(has_below & late_down)(downs[-1].start)
 
         @pl.when(has_above)
         def _():
@@ -331,8 +379,6 @@
             else:
                 add_lags(sums.at[1], from_above, down_at, shifted_down, down_at + rim, down_size)
 
-        if c == len(up_sizes) - 2:
-            pl.when(has_below & ~even)(downs[-1].start)
         up_at += up_size
         down_at += down_size
 
@@ -363,10 +409,13 @@
     line_ref[3:4, :] = east_b
 
     pl.when(has_above)(shift_copy.wait_send)
-    for copy in ups:
-        pl.when(has_above)(copy.wait_send)
-    for copy in downs:
-        pl.when(has_below)(copy.wait_send)
+    for c in range(len(up_sizes)):
+        pl.when(has_above & ~is_low if c == relay else has_above)(ups[c].wait_send)
+        pl.when(has_below & ~is_high if c == relay else has_below)(downs[c].wait_send)
+    pl.when(is_low)(up_leg.wait_send)
+    pl.when(is_high)(down_leg.wait_send)
+    pl.when(is_first)(down_on.wait_send)
+    pl.when(is_last)(up_on.wait_send)
     pl.when(has_east)(to_east.wait_send)
     pl.when(has_west)(to_west.wait_send)
     pl.when(has_west)(info_copy.wait_send)
@@ -470,6 +519,7 @@
             sems((4,)),
             sems((2,)),
             sems((6,)),
+            sems((4,)),
         ],
         compiler_params=pltpu.CompilerParams(collective_id=0, has_side_effects=True),
     )(by_slot, counts, peak_shifts[0], prior)

time: 84.1 us -> 82.6 us (0.982)
  Pallas kernels: 81.8 us -> 80.9 us
    pallas_call x1, Pallas kernels: 80.9 us -> 80 us  [body(): pl.pallas_call(functools.partial(kernel, sections, tiles), in_specs=[pl.B...]
where the time goes in v5:
time: 82.6 us; the launch traced here: 82.2 us
  Pallas kernels  80.9 us (98%)
  between operations  1.28 us (2%)
    pallas_call x1, Pallas kernels, body(): pl.pallas_call(functools.partial(kernel, sections, tiles), in_specs=[pl.B...  80 us

profile of v5, /device:TPU:1, one launch (start us, length us, event | category | flops | bytes accessed | tf_op | source)
XLA Modules:
  0.0 82.2 jit_solution(12112264882738885693)
XLA Ops:
  1.3 80.0 %shard_map.59 = (f32[8,128]{1,0:T(8,128)S(1)}, f32[4,128,128]{2,1,0:T(8,128)S(1)}, bf16[256,256]{1,0:T(8,128)(2,1)S(1)}) custom-call(bf16[160,160,128]{2,1,0:T(8,128)(2,1)} %bitcast.7, s32[1,1]{1,0:T(1,128)S(6)} %copy.6.count_ref, s32[2,128]{1,0:T(2,128)} %bitcast.9, f32[2,128,128]{2,1,0:T(8,128)} %bitcast.8), custom_call_target="tpu_custom_call" | custom-call | tf_op jit(solution)/shard_map/pallas_call | solution.py:478
  81.3 0.8 %shard_map.60 = (f32[2,128]{1,0:T(2,128)}, f32[2,128,128]{2,1,0:T(8,128)}) custom-call(f32[8,128]{1,0:T(8,128)S(1)} %get-tuple-element.7.line_ref, f32[4,128,128]{2,1,0:T(8,128)S(1)} %get-tuple-element.8.base_ref, bf16[256,256]{1,0:T(8,128)(2,1)S(1)} %get-tuple-element.9.owner_ref), custom_call_target="tpu_custom_call" | custom-call | tf_op jit(solution)/shard_map/pallas_call | solution.py:526

commit v6 on v5

--- a/solution.py
+++ b/solution.py
@@ -110,7 +110,7 @@
     count, shift, far_shift, prior, rims, far_rims, fields, goals, gain,
     info, east_info, part_up, part_down, own_up, east_up, east_down,
     local_sem, up_send, up_recv, down_send, down_recv,
-    shift_sem, rim_sem, info_sem, part_sem, relay_sem,
+    shift_sem, rim_sem, info_sem, part_sem, relay_sem, ready,
 ):
     sec, tile = lax.axis_index("sec"), lax.axis_index("tile")
     extent, lanes = local.shape[1:]
@@ -144,9 +144,10 @@
         (has_west, west),
         (has_east, east),
         (is_first, {"sec": middle}),
-        (is_last, {"sec": middle - 1}),
+        (is_last, {"sec": middle}),
     ]
-    greeted = [has_below, has_above, has_west, has_east, is_low, is_high]
+    partners[0] = (has_below & ~is_high, below)
+    greeted = [has_below, has_above & ~is_low, has_west, has_east, is_high, is_high]
 
     def greet(where):
         return lambda: pl.semaphore_signal(
@@ -198,7 +199,7 @@
         )
 
     shift_copy = remote_at(shift_ref, far_shift, shift_sem, 0, above)
-    pl.when(has_above)(shift_copy.start)
+    pl.when(has_above & ~is_low)(shift_copy.start)
     info_copy = remote_at(info, east_info, info_sem, 0, west)
     pl.when(has_west)(info_copy.start)
     to_east = remote_at(rims.at[1], far_rims.at[1], rim_sem, 0, east)
@@ -240,14 +241,26 @@
         relay,
         {"sec": middle - 1},
     )
-    pl.when(is_low)(up_leg.start)
     pl.when(is_high)(down_leg.start)
     for c in range(len(up_sizes)):
-        last = c == len(up_sizes) - 1
-        sends_up = has_above & ~late_up if last else has_above
-        pl.when(sends_up & ~is_low if c == relay else sends_up)(ups[c].start)
-        if not last:
+        sends_up = has_above & ~is_low & ~late_up if c >= relay else has_above & ~is_low
+        pl.when(sends_up)(ups[c].start)
+        if c < len(down_sizes) - 1:
             pl.when(has_below & ~is_high if c == relay else has_below)(downs[c].start)
+
+    @pl.when(is_high)
+    def _():
+        pl.semaphore_signal(ready, 1, device_id=below, device_id_type=MESH)
+
+    @pl.when(is_low)
+    def _():
+        pl.semaphore_wait(ready, 1)
+        shift_copy.start()
+        up_leg.start()
+        for c in range(len(up_sizes)):
+            if c != relay:
+                ups[c].start()
+
     sums[...] = jnp.zeros_like(sums)
     mine[3].wait()
 
@@ -345,42 +358,53 @@
         up_leg.wait_recv()
         up_on.start()
 
-    up_at = down_at = 0
-    for c, (up_size, down_size) in enumerate(zip(up_sizes, down_sizes, strict=True)):
-        final = c == len(up_sizes) - 1
+    up_part = remote_at(part_up, own_up, part_sem, 0, below)
+    up_part_west = remote_at(part_up, east_up, part_sem, 1, below_west)
+
+    def take_up(c):
+        at, size = sum(up_sizes[:c]), up_sizes[c]
 
         @pl.when(has_below)
         def _():
             ups[c].wait_recv()
-            add_lags(sums.at[0], from_below, up_at, shifted_up, up_at, up_size)
-
-        if c == len(up_sizes) - 2:
-            pl.when(has_above & late_up)(ups[-1].start)
-        if final:
-
-            @pl.when(has_below)
-            def _():
-                for k in range(9):
-                    part_up[k : k + 1, :] = jnp.sum(sums[0, k], axis=0, keepdims=True)
-
-            up_part = remote_at(part_up, own_up, part_sem, 0, below)
-            up_part_west = remote_at(part_up, east_up, part_sem, 1, below_west)
-            pl.when(has_below)(up_part.start)
-            pl.when(has_below & has_west)(up_part_west.start)
-
+            add_lags(sums.at[0], from_below, at, shifted_up, at, size)
+
+    def take_down(c):
+        at, size = sum(down_sizes[:c]), down_sizes[c]
+        pl.when(has_above)(downs[c].wait_recv)
         if c == relay:
-            pl.when(has_below & late_down)(downs[-1].start)
+            pl.when(has_below & late_down & ~is_low)(downs[-1].start)
 
         @pl.when(has_above)
         def _():
-            downs[c].wait_recv()
-            if final:
-                add_lags(sums.at[1], from_above, down_at, shifted_rim, 0, down_size)
+            if c == len(down_sizes) - 1:
+                add_lags(sums.at[1], from_above, at, shifted_rim, 0, size)
             else:
-                add_lags(sums.at[1], from_above, down_at, shifted_down, down_at + rim, down_size)
-
-        up_at += up_size
-        down_at += down_size
+                add_lags(sums.at[1], from_above, at, shifted_down, at + rim, size)
+
+    for c in range(relay):
+        take_up(c)
+        take_down(c)
+    pl.when(has_above & late_up)(ups[relay].start)
+    pl.when(has_above & late_up)(ups[-1].start)
+    take_down(relay)
+
+    @pl.when(late_down & is_low)
+    def _():
+        downs[relay].wait_send()
+        downs[-1].start()
+
+    take_up(relay)
+    take_up(relay + 1)
+
+    @pl.when(has_below)
+    def _():
+        for k in range(9):
+            part_up[k : k + 1, :] = jnp.sum(sums[0, k], axis=0, keepdims=True)
+
+    pl.when(has_below & has_west)(up_part_west.start)
+    pl.when(has_below)(up_part.start)
+    take_down(relay + 1)
 
     for k in range(9):
         part_down[k : k + 1, :] = jnp.sum(sums[1, 8 - k], axis=0, keepdims=True)
@@ -411,7 +435,8 @@
     pl.when(has_above)(shift_copy.wait_send)
     for c in range(len(up_sizes)):
         pl.when(has_above & ~is_low if c == relay else has_above)(ups[c].wait_send)
-        pl.when(has_below & ~is_high if c == relay else has_below)(downs[c].wait_send)
+        sent_down = has_below & ~is_high & ~(late_down & is_low) if c == relay else has_below
+        pl.when(sent_down)(downs[c].wait_send)
     pl.when(is_low)(up_leg.wait_send)
     pl.when(is_high)(down_leg.wait_send)
     pl.when(is_first)(down_on.wait_send)
@@ -520,6 +545,7 @@
             sems((2,)),
             sems((6,)),
             sems((4,)),
+            pltpu.SemaphoreType.REGULAR,
         ],
         compiler_params=pltpu.CompilerParams(collective_id=0, has_side_effects=True),
     )(by_slot, counts, peak_shifts[0], prior)

time: 82.6 us -> 81.5 us (0.987)
  no operation moved by 1% of the time
where the time goes in v6:
time: 81.5 us; the launch traced here: 81.4 us
  Pallas kernels  80.1 us (98%)
  between operations  1.28 us (2%)
    pallas_call x1, Pallas kernels, body(): pl.pallas_call(functools.partial(kernel, sections, tiles), in_specs=[pl.B...  79.2 us

profile of v6, /device:TPU:1, one launch (start us, length us, event | category | flops | bytes accessed | tf_op | source)
XLA Modules:
  0.0 81.4 jit_solution(12813726494758773058)
XLA Ops:
  1.3 79.2 %shard_map.59 = (f32[8,128]{1,0:T(8,128)S(1)}, f32[4,128,128]{2,1,0:T(8,128)S(1)}, bf16[256,256]{1,0:T(8,128)(2,1)S(1)}) custom-call(bf16[160,160,128]{2,1,0:T(8,128)(2,1)} %bitcast.7, s32[1,1]{1,0:T(1,128)S(6)} %copy.6.count_ref, s32[2,128]{1,0:T(2,128)} %bitcast.9, f32[2,128,128]{2,1,0:T(8,128)} %bitcast.8), custom_call_target="tpu_custom_call" | custom-call | tf_op jit(solution)/shard_map/pallas_call | solution.py:503
  80.5 0.8 %shard_map.60 = (f32[2,128]{1,0:T(2,128)}, f32[2,128,128]{2,1,0:T(8,128)}) custom-call(f32[8,128]{1,0:T(8,128)S(1)} %get-tuple-element.7.line_ref, f32[4,128,128]{2,1,0:T(8,128)S(1)} %get-tuple-element.8.base_ref, bf16[256,256]{1,0:T(8,128)(2,1)S(1)} %get-tuple-element.9.owner_ref), custom_call_target="tpu_custom_call" | custom-call | tf_op jit(solution)/shard_map/pallas_call | solution.py:552

commit v7 on v6

--- a/solution.py
+++ b/solution.py
@@ -105,7 +105,7 @@
 def kernel(
     sections, tiles,
     patch_ref, count_ref, shift_ref, prior_ref,
-    line_ref, base_ref, owner_ref,
+    line_ref, base_ref,
     local, merged, from_above, from_below, shifted_up, shifted_down, shifted_rim, temp, sums,
     count, shift, far_shift, prior, rims, far_rims, fields, goals, gain,
     info, east_info, part_up, part_down, own_up, east_up, east_down,
@@ -128,6 +128,7 @@
     is_low, is_high = sec == middle - 1, sec == middle
     is_first, is_last = sec == 0, sec == sections - 1
     late_up, late_down = ~even & ~is_low, ~even & ~is_high
+    own_pace = is_low | is_last
 
     far_rims[...] = jnp.zeros_like(far_rims)
     line_ref[...] = jnp.zeros_like(line_ref)
@@ -339,15 +340,6 @@
     lax.fori_loop(0, ITERS, sweep, 0)
     for k in range(4):
         base_ref[k] = fields[k, :, :cols]
-    owner_ref[...] = slot_places(
-        2 * cols, lanes, cols, PCOLS,
-        lambda lane: jnp.where(
-            lane < cols,
-            2 * ((lane + col_step) // (2 * col_step)),
-            2 * ((lane - cols) // (2 * col_step)) + 1,
-        ),
-    )
-
     @pl.when(is_first)
     def _():
         down_leg.wait_recv()
@@ -373,7 +365,7 @@
         at, size = sum(down_sizes[:c]), down_sizes[c]
         pl.when(has_above)(downs[c].wait_recv)
         if c == relay:
-            pl.when(has_below & late_down & ~is_low)(downs[-1].start)
+            pl.when(late_down & ~own_pace & has_below)(downs[-1].start)
 
         @pl.when(has_above)
         def _():
@@ -389,7 +381,7 @@
     pl.when(has_above & late_up)(ups[-1].start)
     take_down(relay)
 
-    @pl.when(late_down & is_low)
+    @pl.when(late_down & own_pace)
     def _():
         downs[relay].wait_send()
         downs[-1].start()
@@ -435,7 +427,7 @@
     pl.when(has_above)(shift_copy.wait_send)
     for c in range(len(up_sizes)):
         pl.when(has_above & ~is_low if c == relay else has_above)(ups[c].wait_send)
-        sent_down = has_below & ~is_high & ~(late_down & is_low) if c == relay else has_below
+        sent_down = has_below & ~is_high & ~(late_down & own_pace) if c == relay else has_below
         pl.when(sent_down)(downs[c].wait_send)
     pl.when(is_low)(up_leg.wait_send)
     pl.when(is_high)(down_leg.wait_send)
@@ -449,9 +441,19 @@
     pl.when(has_west)(down_part.wait_send)
 
 
-def finish_kernel(line_ref, base_ref, owner_ref, flow_ref, out_ref):
+def finish_kernel(line_ref, base_ref, flow_ref, out_ref):
     rows, cols = base_ref.shape[1:]
-    patch_rows = line_ref.shape[1] // PCOLS
+    lanes = line_ref.shape[1]
+    patch_rows, col_step = lanes // PCOLS, cols // PCOLS
+    owners = slot_places(
+        2 * cols, lanes, cols, PCOLS,
+        lambda lane: jnp.where(
+            lane < cols,
+            2 * ((lane + col_step) // (2 * col_step)),
+            2 * ((lane - cols) // (2 * col_step)) + 1,
+        ),
+    )
+
     step = rows // patch_rows
     flow_ref[...] = line_ref[0:2, :]
     left = jnp.concatenate(
@@ -468,7 +470,7 @@
     second = rest.astype(jnp.bfloat16)
     third = (rest - second.astype(jnp.float32)).astype(jnp.bfloat16)
     parts = jnp.dot(
-        jnp.concatenate([first, second, third], 0), owner_ref[...], preferred_element_type=jnp.float32
+        jnp.concatenate([first, second, third], 0), owners, preferred_element_type=jnp.float32
     )
     size = 2 * patch_rows
     values = parts[:size] + parts[size : 2 * size] + parts[2 * size :]
@@ -500,14 +502,13 @@
     sems = pltpu.SemaphoreType.DMA
     vmem = pl.BlockSpec(memory_space=pltpu.VMEM)
     f32, bf16 = jnp.float32, jnp.bfloat16
-    lines, base, owners = pl.pallas_call(
+    lines, base = pl.pallas_call(
         functools.partial(kernel, sections, tiles),
         in_specs=[pl.BlockSpec(memory_space=pltpu.HBM)] * 4,
-        out_specs=[vmem, vmem, vmem],
+        out_specs=[vmem, vmem],
         out_shape=[
             pltpu.VMEM((8, slots), f32),
             pltpu.VMEM((4, rows, cols), f32),
-            pltpu.VMEM((2 * slots, 2 * cols), bf16),
         ],
         scratch_shapes=[
             pltpu.VMEM(by_slot.shape, bf16),
@@ -551,13 +552,13 @@
     )(by_slot, counts, peak_shifts[0], prior)
     flows, displacement = pl.pallas_call(
         finish_kernel,
-        in_specs=[vmem, vmem, vmem],
+        in_specs=[vmem, vmem],
         out_specs=[vmem, vmem],
         out_shape=[
             jax.ShapeDtypeStruct((2, slots), f32),
             jax.ShapeDtypeStruct(prior.shape, f32),
         ],
-    )(*[pltpu.with_memory_space_constraint(x, pltpu.VMEM) for x in (lines, base, owners)])
+    )(*[pltpu.with_memory_space_constraint(x, pltpu.VMEM) for x in (lines, base)])
     return flows[None], displacement[None, None]
 
 

time: 81.5 us -> 81.5 us (level)
  no operation moved by 1% of the time
where the time goes in v7:
time: 81.5 us; the launch traced here: 81.4 us
  Pallas kernels  80.1 us (98%)
  between operations  1.28 us (2%)
    pallas_call x1, Pallas kernels, body(): pl.pallas_call(functools.partial(kernel, sections, tiles), in_specs=[pl.B...  79.2 us

profile of v7, /device:TPU:1, one launch (start us, length us, event | category | flops | bytes accessed | tf_op | source)
XLA Modules:
  0.0 81.4 jit_solution(16038374110750704333)
XLA Ops:
  1.3 79.2 %shard_map.59 = (f32[8,128]{1,0:T(8,128)S(1)}, f32[4,128,128]{2,1,0:T(8,128)S(1)}) custom-call(bf16[160,160,128]{2,1,0:T(8,128)(2,1)} %bitcast.7, s32[1,1]{1,0:T(1,128)S(6)} %copy.6.count_ref, s32[2,128]{1,0:T(2,128)} %bitcast.9, f32[2,128,128]{2,1,0:T(8,128)} %bitcast.8), custom_call_target="tpu_custom_call" | custom-call | tf_op jit(solution)/shard_map/pallas_call | solution.py:505
  80.5 0.8 %shard_map.60 = (f32[2,128]{1,0:T(2,128)}, f32[2,128,128]{2,1,0:T(8,128)}) custom-call(f32[8,128]{1,0:T(8,128)S(1)} %get-tuple-element.6.line_ref, f32[4,128,128]{2,1,0:T(8,128)S(1)} %get-tuple-element.7.base_ref), custom_call_target="tpu_custom_call" | custom-call | tf_op jit(solution)/shard_map/pallas_call | solution.py:553

commit v8 on v7

--- a/solution.py
+++ b/solution.py
@@ -166,21 +166,6 @@
     ]
     for copy in mine:
         copy.start()
-    mine[0].wait()
-    mine[1].wait()
-    alive = jnp.where(
-        lax.broadcasted_iota(jnp.int32, (1, lanes), 1) < count[0, 0], 1.0, 0.0
-    )
-    row_shift = shift[0:1, :].astype(jnp.float32)
-    col_shift = shift[1:2, :].astype(jnp.float32)
-    info[0:1, :] = row_shift
-    info[1:2, :] = col_shift
-    info[2:3, :] = alive
-    mine[2].wait()
-    for k in range(2):
-        turned = jnp.transpose(prior[k])
-        rims[0, k] = turned[:ITERS]
-        rims[1, k] = turned[cols - ITERS :]
     pl.semaphore_wait(barrier, waits)
 
     def remote(src, dst, sems, k, where):
@@ -201,12 +186,6 @@
 
     shift_copy = remote_at(shift_ref, far_shift, shift_sem, 0, above)
     pl.when(has_above & ~is_low)(shift_copy.start)
-    info_copy = remote_at(info, east_info, info_sem, 0, west)
-    pl.when(has_west)(info_copy.start)
-    to_east = remote_at(rims.at[1], far_rims.at[1], rim_sem, 0, east)
-    to_west = remote_at(rims.at[0], far_rims.at[0], rim_sem, 1, west)
-    pl.when(has_east)(to_east.start)
-    pl.when(has_west)(to_west.start)
     ups, downs = [], []
     at = 0
     for c, size in enumerate(up_sizes):
@@ -248,6 +227,28 @@
         pl.when(sends_up)(ups[c].start)
         if c < len(down_sizes) - 1:
             pl.when(has_below & ~is_high if c == relay else has_below)(downs[c].start)
+
+    mine[0].wait()
+    mine[1].wait()
+    alive = jnp.where(
+        lax.broadcasted_iota(jnp.int32, (1, lanes), 1) < count[0, 0], 1.0, 0.0
+    )
+    row_shift = shift[0:1, :].astype(jnp.float32)
+    col_shift = shift[1:2, :].astype(jnp.float32)
+    info[0:1, :] = row_shift
+    info[1:2, :] = col_shift
+    info[2:3, :] = alive
+    mine[2].wait()
+    for k in range(2):
+        turned = jnp.transpose(prior[k])
+        rims[0, k] = turned[:ITERS]
+        rims[1, k] = turned[cols - ITERS :]
+    info_copy = remote_at(info, east_info, info_sem, 0, west)
+    pl.when(has_west)(info_copy.start)
+    to_east = remote_at(rims.at[1], far_rims.at[1], rim_sem, 0, east)
+    to_west = remote_at(rims.at[0], far_rims.at[0], rim_sem, 1, west)
+    pl.when(has_east)(to_east.start)
+    pl.when(has_west)(to_west.start)
 
     @pl.when(is_high)
     def _():

time: 81.5 us -> 81.3 us (level)
  no operation moved by 1% of the time
where the time goes in v8:
time: 81.3 us; the launch traced here: 81.2 us
  Pallas kernels  79.9 us (98%)
  between operations  1.28 us (2%)
    pallas_call x1, Pallas kernels, body(): pl.pallas_call(functools.partial(kernel, sections, tiles), in_specs=[pl.B...  79.1 us

profile of v8, /device:TPU:1, one launch (start us, length us, event | category | flops | bytes accessed | tf_op | source)
XLA Modules:
  0.0 81.2 jit_solution(2892758626254406358)
XLA Ops:
  1.3 79.1 %shard_map.59 = (f32[8,128]{1,0:T(8,128)S(1)}, f32[4,128,128]{2,1,0:T(8,128)S(1)}) custom-call(bf16[160,160,128]{2,1,0:T(8,128)(2,1)} %bitcast.7, s32[1,1]{1,0:T(1,128)S(6)} %copy.6.count_ref, s32[2,128]{1,0:T(2,128)} %bitcast.9, f32[2,128,128]{2,1,0:T(8,128)} %bitcast.8), custom_call_target="tpu_custom_call" | custom-call | tf_op jit(solution)/shard_map/pallas_call | solution.py:506
  80.3 0.8 %shard_map.60 = (f32[2,128]{1,0:T(2,128)}, f32[2,128,128]{2,1,0:T(8,128)}) custom-call(f32[8,128]{1,0:T(8,128)S(1)} %get-tuple-element.6.line_ref, f32[4,128,128]{2,1,0:T(8,128)S(1)} %get-tuple-element.7.base_ref), custom_call_target="tpu_custom_call" | custom-call | tf_op jit(solution)/shard_map/pallas_call | solution.py:554
